TPU v7x, 256 devices: a whole 4x4x8 slice. The times are simulated.
256 devices in a mesh: dom: 16 (over z, core), sub: 16 (over y, x).
Axes of the slice: x: 4, y: 4, z: 8, core: 2. Of those that a mesh axis runs over, the one named last changes fastest.
Arguments:
- start_fields: float32 [4, 512, 128, 128], P(None, 'dom', 'sub'), may hold values from -6 to 6
- source: float32 [2, 512, 128, 128], P(None, 'dom', 'sub'), may hold values from -4 to 4
- labels: int32 [512, 128, 128], P('dom', 'sub'), may hold values from 0 to 15
- wavenumber2: float32 [16], replicated, may hold values from 0.05 to 0.4
- absorption: float32 [16], replicated, may hold values from 1.5 to 8
- design_weight: float32 [16], replicated, may hold values from 0.2 to 1.5
- pairs: int32 [16, 16, 1024], P('dom', 'sub'), may hold values from 0 to 1023, each once within a row
- block_index: int32 [16, 16], P('dom'), may hold values from 0 to 15
- blocks: bfloat16 [16, 16, 2, 1024, 1024], P('dom', 'sub'), may hold values from -0.103125 to 0.703125, as said below
Outputs:
- forward: float32 [2, 512, 128, 128], P(None, 'dom', 'sub')
- adjoint: float32 [2, 512, 128, 128], P(None, 'dom', 'sub')
Inputs may be any that keep to these rules, and one draw needn't show every extreme that they name: `pairs`: each row is a one-to-one pairing of the 1024 points of a patch; the rows of the last subdomain are not read. `block_index`: several patches may use the same block. `blocks`: index 0 of the third dimension is a block's real part, index 1 its imaginary part.
All inputs are finite; a program needn't handle non-finite values.
Results may differ from a plain program's by a relative error of at most 0.0029.
Values may be sent and summed in bfloat16 or wider, within the bound.
A program may use at most 192 MiB of HBM per device.

v0:
```python
import jax
import jax.numpy as jnp
from jax import lax
from jax.sharding import PartitionSpec as P

SWEEPS = 4
ITERS = 2


def from_behind(array, axis, by):
    length = lax.axis_size(axis)
    pairs = [(i, i + by) for i in range(length) if 0 <= i + by < length]
    return lax.ppermute(array, axis, pairs)


def with_halo(block, sides, width):
    for axis, dim in sides:
        count = lax.axis_size(axis)
        forward = [(i, i + 1) for i in range(count - 1)]
        backward = [(target, source) for source, target in forward]
        low = lax.ppermute(
            lax.slice_in_dim(block, block.shape[dim] - width, None, axis=dim), axis, forward
        )
        high = lax.ppermute(lax.slice_in_dim(block, 0, width, axis=dim), axis, backward)
        block = jnp.concatenate([low, block, high], axis=dim)
    return block


def lookup(table, labels):
    materials = jnp.arange(table.shape[0], dtype=jnp.int32)
    match_mask = labels[None] == materials[:, None, None, None]
    return jnp.sum(jnp.where(match_mask, table[:, None, None, None], 0.0), axis=0)


def relax_step(fields, neighbours, coefficient_stack):
    recip_real = coefficient_stack[0]
    recip_imag = coefficient_stack[1]
    weight = coefficient_stack[4]
    forward_real = coefficient_stack[2] + neighbours[0]
    forward_imag = coefficient_stack[3] + neighbours[1]
    adjoint_real = weight * fields[0] + neighbours[2]
    adjoint_imag = weight * fields[1] + neighbours[3]
    return jnp.stack(
        [
            recip_real * forward_real - recip_imag * forward_imag,
            recip_real * forward_imag + recip_imag * forward_real,
            recip_real * adjoint_real + recip_imag * adjoint_imag,
            recip_real * adjoint_imag - recip_imag * adjoint_real,
        ]
    )


def neighbour_sum(fields, across, beside_rows):
    z_padded = jnp.pad(fields, ((0, 0), (0, 0), (0, 0), (1, 1)))
    return (
        across[:, 2:]
        + across[:, :-2]
        + (beside_rows[:, :, 2:] + beside_rows[:, :, :-2])
        + (z_padded[..., 2:] + z_padded[..., :-2])
    )


def products(row_block, matrix_pair):
    contract = (((1,), (1,)), ((), ()))
    real_part = lax.dot_general(
        row_block, matrix_pair[0], contract, preferred_element_type=jnp.float32
    )
    imag_part = lax.dot_general(
        row_block, matrix_pair[1], contract, preferred_element_type=jnp.float32
    )
    return (real_part, imag_part)


def combine(real_part, imag_part):
    row_total = real_part.shape[0]
    real_four = real_part.reshape(row_total // 4, 4, real_part.shape[1])
    imag_four = imag_part.reshape(row_total // 4, 4, imag_part.shape[1])
    joined = jnp.stack(
        [
            real_four[:, 0] - imag_four[:, 1],
            real_four[:, 1] + imag_four[:, 0],
            real_four[:, 2] - imag_four[:, 3],
            real_four[:, 3] + imag_four[:, 2],
        ],
        axis=1,
    )
    return joined.reshape(row_total, real_part.shape[1])


def per_device(
    start_fields, source, labels, wavenumber2, absorption, design_weight, pairs, block_index, blocks
):
    patch_size = pairs.shape[-1]
    rows_here = labels.shape[1]
    wave_sq = lookup(wavenumber2, labels)
    damping = lookup(absorption, labels)
    weight = lookup(design_weight, labels)
    shifted = 6.0 - wave_sq
    modulus = shifted * shifted + damping * damping
    coefficient_stack = jnp.stack(
        [shifted / modulus, damping / modulus, source[0], source[1], weight]
    )
    facing_order = pairs[0, 0]
    inverse = (
        jnp.zeros((patch_size,), jnp.int32)
        .at[facing_order]
        .set(jnp.arange(patch_size, dtype=jnp.int32))
    )
    owners = block_index[0]
    member = lax.axis_index("sub")
    is_last = lax.axis_index("dom") == lax.axis_size("dom") - 1
    library = lax.all_gather(blocks, "sub", axis=1, tiled=True)
    chosen = lax.dynamic_index_in_dim(library[0], jnp.take(owners, member), 0, keepdims=False)
    fields = start_fields
    ghost_shape = (4, 1, rows_here, patch_size // rows_here)
    for iteration in range(ITERS):
        left_trace = fields[:, 0].reshape(4, patch_size)
        right_trace = fields[:, -1].reshape(4, patch_size)
        following = from_behind(left_trace, "dom", -1)
        facing = jnp.take(following, facing_order, axis=1)
        jump_data = (facing - right_trace).astype(jnp.bfloat16)
        real_part, imag_part = products(jump_data, chosen)
        transmitted = combine(real_part, imag_part)
        right_ghost = jnp.where(is_last, 0.0, facing + transmitted).reshape(ghost_shape)
        returned = jnp.take(right_trace - transmitted, inverse, axis=1)
        left_ghost = from_behind(returned, "dom", 1).reshape(ghost_shape)
        for sweep_index in range(SWEEPS):
            beside_rows = with_halo(fields, (("sub", 2),), 1)
            across = jnp.concatenate([left_ghost, fields, right_ghost], axis=1)
            fields = relax_step(
                fields, neighbour_sum(fields, across, beside_rows), coefficient_stack
            )
    return (fields[0:2], fields[2:4])


def solution(mesh):
    placed = (
        P(None, "dom", "sub", None),
        P(None, "dom", "sub", None),
        P("dom", "sub", None),
        P(),
        P(),
        P(),
        P("dom", "sub", None),
        P("dom", None),
        P("dom", "sub", None, None, None),
    )
    return jax.shard_map(
        per_device,
        mesh=mesh,
        in_specs=placed,
        out_specs=(P(None, "dom", "sub", None), P(None, "dom", "sub", None)),
        check_vma=False,
    )
```

profile of v0, /device:TPU:1, one launch (start us, length us, event | category | flops | bytes accessed | tf_op | source)
XLA Modules:
  0.0 507.4 jit_solution(12314383954674353123)
XLA Ops:
  7.2 0.7 all-gather.2.cloned.1.call-update
  8.5 5.1 %collective-permute-start = (f32[4,1024]{0,1:T(8,128)S(1)}, f32[4,1024]{0,1:T(8,128)S(1)}, u32[]{:S(2)}, u32[]{:S(2)}) collective-permute-start(f32[4,1024]{0,1:T(8,128)S(1)} %bitcast.248), channel_id=1, source_target_pairs={{16,0},{32,16},{48,32},{64,48},{80,64},{96,80},{112,96},{128,112},... | collective-permute-start | bytes 49160 | tf_op jit(solution)/shard_map/ppermute | solution.py:13
  13.7 1.4 collective-permute-start.3
  15.1 1.3 collective-permute-start.2
  16.5 4.3 scatter_custom_fusion
  20.9 0.6 constant_dynamic-slice_fusion
  22.1 2.8 gather_fusion
  25.1 362.5 %all-gather.2.cloned.1.call-done = bf16[1,16,2,1024,1024]{4,3,2,0,1:T(8,128)(2,1)} async-done(((bf16[1,1,2,1024,1024]{4,3,2,0,1:T(8,128)(2,1)}), bf16[1,16,2,1024,1024]{4,3,2,0,1:T(8,128)(2,1)}) %all-gather.2.cloned.1.call-update) | async-done | bytes 67108880 | tf_op jit(solution)/shard_map/all_gather | solution.py:112
  387.6 2.2 fusion.6
  389.9 2.3 fusion.4
  392.5 2.8 gather_fusion.1
  395.5 3.9 collective-permute-start.1
  399.4 0.5 select_reduce_fusion
  400.0 5.5 %collective-permute-done.1 = f32[4,1024]{0,1:T(8,128)S(1)} collective-permute-done((f32[4,1024]{0,1:T(8,128)S(1)}, f32[4,1024]{0,1:T(8,128)S(1)}, u32[]{:S(2)}, u32[]{:S(2)}) %collective-permute-start.1) | collective-permute-done | bytes 16416 | tf_op jit(solution)/shard_map/ppermute | solution.py:13
  405.7 0.4 fusion.10
  406.4 3.1 collective-permute-start.5
  409.5 1.3 collective-permute-start.4
  410.8 3.7 collective-permute-done.4
  414.5 0.4 fusion.13
  415.1 3.1 collective-permute-start.7
  418.2 1.3 collective-permute-start.6
  419.5 3.7 collective-permute-done.6
  423.9 4.6 collective-permute-start.9
  428.5 1.3 collective-permute-start.8
  429.8 3.7 collective-permute-done.8
  433.5 0.4 fusion.19
  434.2 1.9 collective-permute-start.10
  436.3 4.0 collective-permute-start.13
  440.3 1.3 collective-permute-start.12
  441.6 8.0 %collective-permute-done.10 = f32[4,1024]{0,1:T(8,128)} collective-permute-done((f32[4,1024]{0,1:T(8,128)S(1)}, f32[4,1024]{0,1:T(8,128)}, u32[]{:S(2)}, u32[]{:S(2)}) %collective-permute-start.10) | collective-permute-done | bytes 16416 | tf_op jit(solution)/shard_map/ppermute | solution.py:13
  449.6 3.8 gather_fusion.2
  453.7 2.2 fusion.5
  455.9 2.2 fusion.7
  458.5 2.8 gather_fusion.3
  461.5 1.9 collective-permute-start.11
  463.4 6.1 %collective-permute-done.11 = f32[4,1024]{0,1:T(8,128)S(1)} collective-permute-done((f32[4,1024]{0,1:T(8,128)S(1)}, f32[4,1024]{0,1:T(8,128)S(1)}, u32[]{:S(2)}, u32[]{:S(2)}) %collective-permute-start.11) | collective-permute-done | bytes 16416 | tf_op jit(solution)/shard_map/ppermute | solution.py:13
  470.3 3.7 collective-permute-start.15
  474.1 1.3 collective-permute-start.14
  475.4 4.0 collective-permute-done.14
  479.4 0.4 fusion.25
  480.0 3.8 collective-permute-start.17
  483.8 1.3 collective-permute-start.16
  485.1 3.7 collective-permute-done.16
  488.8 0.4 fusion.28
  489.4 4.9 collective-permute-start.19
  494.3 1.3 collective-permute-start.18
  495.6 3.7 collective-permute-done.18
  499.8 0.8 pad_maximum_fusion.123
  (81 shorter events, 5.7 us)
Async XLA Ops:
  7.2 13.7 %copy-start = (s32[1,16]{1,0:T(1,128)S(1)}, s32[1,16]{1,0:T(1,128)}, u32[]{:S(2)}) copy-start(s32[1,16]{1,0:T(1,128)} %param.18) | copy-start | bytes 196
  7.2 380.4 %all-gather.2.cloned.1.call-start = ((), (), s32[]{:S(2)}) async-start(), calls=%async_computation | async-start | bytes 71303168 | tf_op jit(solution)/shard_map/all_gather | solution.py:112
  7.2 1.0 copy-start.2
  7.2 9.2 %copy-start.4 = (s32[1,1,1024]{2,1,0:T(1,128)S(1)}, s32[1,1,1024]{2,1,0:T(1,128)}, u32[]{:S(2)}) copy-start(s32[1,1,1024]{2,1,0:T(1,128)} %param.17) | copy-start | bytes 12292
  8.5 13.6 %collective-permute-start = (f32[4,1024]{0,1:T(8,128)S(1)}, f32[4,1024]{0,1:T(8,128)S(1)}, u32[]{:S(2)}, u32[]{:S(2)}) collective-permute-start(f32[4,1024]{0,1:T(8,128)S(1)} %bitcast.248), channel_id=1, source_target_pairs={{16,0},{32,16},{48,32},{64,48},{80,64},{96,80},{112,96},{128,112},... | collective-permute-start | bytes 49160 | tf_op jit(solution)/shard_map/ppermute | solution.py:13
  13.7 392.0 %collective-permute-start.3 = (f32[4,32,1,128]{3,2,1,0:T(1,128)S(1)}, f32[4,32,1,128]{3,2,1,0:T(1,128)S(1)}, u32[]{:S(2)}, u32[]{:S(2)}) collective-permute-start(f32[4,32,1,128]{3,2,1,0:T(1,128)S(1)} %get-tuple-element.82), channel_id=1, source_target_pairs={{0,1},{1,2},{2,3},{3,4},{4,5},{5,6},{6,7},{7,8},{8,9},{9,10},{10,1... | collective-permute-start | bytes 196616 | tf_op jit(solution)/shard_map/ppermute | solution.py:21
  15.1 390.6 %collective-permute-start.2 = (f32[4,32,1,128]{3,2,1,0:T(1,128)S(1)}, f32[4,32,1,128]{3,2,1,0:T(1,128)S(1)}, u32[]{:S(2)}, u32[]{:S(2)}) collective-permute-start(f32[4,32,1,128]{3,2,1,0:T(1,128)S(1)} %get-tuple-element.81), channel_id=1, source_target_pairs={{1,0},{2,1},{3,2},{4,3},{5,4},{6,5},{7,6},{8,7},{9,8},{10,9},{11,1... | collective-permute-start | bytes 196616 | tf_op jit(solution)/shard_map/ppermute | solution.py:24
  389.8 9.6 %copy-start.3 = (s32[32,8,128]{2,1,0:T(8,128)S(1)}, s32[32,8,128]{2,1,0:T(8,128)}, u32[]{:S(2)}) copy-start(s32[32,8,128]{2,1,0:T(8,128)} %param.13) | copy-start | bytes 393220
  389.8 9.6 %copy-start.5 = (f32[16]{0:T(128)S(1)}, f32[16]{0:T(128)}, u32[]{:S(2)}) copy-start(f32[16]{0:T(128)} %param.16) | copy-start | bytes 196
  389.8 9.6 %copy-start.6 = (f32[16]{0:T(128)S(1)}, f32[16]{0:T(128)}, u32[]{:S(2)}) copy-start(f32[16]{0:T(128)} %param.15) | copy-start | bytes 196
  389.9 9.6 %copy-start.7 = (f32[16]{0:T(128)S(1)}, f32[16]{0:T(128)}, u32[]{:S(2)}) copy-start(f32[16]{0:T(128)} %param.14) | copy-start | bytes 196
  392.1 13.9 %copy-start.1 = (f32[2,32,8,128]{3,2,1,0:T(8,128)S(1)}, f32[2,32,8,128]{3,2,1,0:T(8,128)}, u32[]{:S(2)}) copy-start(f32[2,32,8,128]{3,2,1,0:T(8,128)} %param.12) | copy-start | bytes 786436
  395.5 10.0 %collective-permute-start.1 = (f32[4,1024]{0,1:T(8,128)S(1)}, f32[4,1024]{0,1:T(8,128)S(1)}, u32[]{:S(2)}, u32[]{:S(2)}) collective-permute-start(f32[4,1024]{0,1:T(8,128)S(1)} %select_bitcast_fusion.1), channel_id=1, source_target_pairs={{0,16},{16,32},{32,48},{48,64},{64,80},{80,96},{96,112},{112,128},... | collective-permute-start | bytes 49160 | tf_op jit(solution)/shard_map/ppermute | solution.py:13
  406.4 4.4 collective-permute-start.5
  409.5 5.0 collective-permute-start.4
  415.1 4.4 collective-permute-start.7
  418.2 5.0 collective-permute-start.6
  423.9 5.9 %collective-permute-start.9 = (f32[4,32,1,128]{3,2,1,0:T(1,128)S(1)}, f32[4,32,1,128]{3,2,1,0:T(1,128)S(1)}, u32[]{:S(2)}, u32[]{:S(2)}) collective-permute-start(f32[4,32,1,128]{3,2,1,0:T(1,128)S(1)} %get-tuple-element.76), channel_id=1, source_target_pairs={{0,1},{1,2},{2,3},{3,4},{4,5},{5,6},{6,7},{7,8},{8,9},{9,10},{10,1... | collective-permute-start | bytes 196616 | tf_op jit(solution)/shard_map/ppermute | solution.py:21
  428.5 5.0 collective-permute-start.8
  434.2 15.4 %collective-permute-start.10 = (f32[4,1024]{0,1:T(8,128)S(1)}, f32[4,1024]{0,1:T(8,128)}, u32[]{:S(2)}, u32[]{:S(2)}) collective-permute-start(f32[4,1024]{0,1:T(8,128)S(1)} %bitcast.249), channel_id=1, source_target_pairs={{16,0},{32,16},{48,32},{64,48},{80,64},{96,80},{112,96},{128,112},... | collective-permute-start | bytes 49160 | tf_op jit(solution)/shard_map/ppermute | solution.py:13
  436.3 33.5 %collective-permute-start.13 = (f32[4,32,1,128]{3,2,1,0:T(1,128)S(1)}, f32[4,32,1,128]{3,2,1,0:T(1,128)S(1)}, u32[]{:S(2)}, u32[]{:S(2)}) collective-permute-start(f32[4,32,1,128]{3,2,1,0:T(1,128)S(1)} %get-tuple-element.72), channel_id=1, source_target_pairs={{0,1},{1,2},{2,3},{3,4},{4,5},{5,6},{6,7},{7,8},{8,9},{9,10},{10,1... | collective-permute-start | bytes 196616 | tf_op jit(solution)/shard_map/ppermute | solution.py:21
  440.3 29.4 %collective-permute-start.12 = (f32[4,32,1,128]{3,2,1,0:T(1,128)S(1)}, f32[4,32,1,128]{3,2,1,0:T(1,128)S(1)}, u32[]{:S(2)}, u32[]{:S(2)}) collective-permute-start(f32[4,32,1,128]{3,2,1,0:T(1,128)S(1)} %get-tuple-element.71), channel_id=1, source_target_pairs={{1,0},{2,1},{3,2},{4,3},{5,4},{6,5},{7,6},{8,7},{9,8},{10,9},{11,1... | collective-permute-start | bytes 196616 | tf_op jit(solution)/shard_map/ppermute | solution.py:24
  461.5 8.0 %collective-permute-start.11 = (f32[4,1024]{0,1:T(8,128)S(1)}, f32[4,1024]{0,1:T(8,128)S(1)}, u32[]{:S(2)}, u32[]{:S(2)}) collective-permute-start(f32[4,1024]{0,1:T(8,128)S(1)} %select_bitcast_fusion), channel_id=1, source_target_pairs={{0,16},{16,32},{32,48},{48,64},{64,80},{80,96},{96,112},{112,128},... | collective-permute-start | bytes 49160 | tf_op jit(solution)/shard_map/ppermute | solution.py:13
  470.3 5.1 collective-permute-start.15
  474.1 5.3 %collective-permute-start.14 = (f32[4,32,1,128]{3,2,1,0:T(1,128)S(1)}, f32[4,32,1,128]{3,2,1,0:T(1,128)S(1)}, u32[]{:S(2)}, u32[]{:S(2)}) collective-permute-start(f32[4,32,1,128]{3,2,1,0:T(1,128)S(1)} %get-tuple-element.69), channel_id=1, source_target_pairs={{1,0},{2,1},{3,2},{4,3},{5,4},{6,5},{7,6},{8,7},{9,8},{10,9},{11,1... | collective-permute-start | bytes 196616 | tf_op jit(solution)/shard_map/ppermute | solution.py:24
  480.0 5.1 collective-permute-start.17
  483.8 5.0 collective-permute-start.16
  489.4 6.2 %collective-permute-start.19 = (f32[4,32,1,128]{3,2,1,0:T(1,128)S(1)}, f32[4,32,1,128]{3,2,1,0:T(1,128)S(1)}, u32[]{:S(2)}, u32[]{:S(2)}) collective-permute-start(f32[4,32,1,128]{3,2,1,0:T(1,128)S(1)} %get-tuple-element.66), channel_id=1, source_target_pairs={{0,1},{1,2},{2,3},{3,4},{4,5},{5,6},{6,7},{7,8},{8,9},{9,10},{10,1... | collective-permute-start | bytes 196616 | tf_op jit(solution)/shard_map/ppermute | solution.py:21
  494.3 5.0 collective-permute-start.18
Sparse Core Ops, SparseCore 0:
  10.4 377.1 all-gather.1
where the time goes:
time: 515 us; the launch traced here: 507 us
  waiting for transfers between devices  405 us (79%)
  starting transfers between devices  51.8 us (10%)
  local copies, waits for them, and re-layouts  19.9 us (4%)
  between operations  15.4 us (3%)
  matrix products  8.99 us (2%)
  other arithmetic  6.14 us (1%)
    all_gather x1, waiting for transfers between devices, per_device(): library = lax.all_gather(blocks, 'sub', axis=1, tiled=True)  362 us
    ppermute x8, starting transfers between devices, with_halo(): lax.ppermute(lax.slice_in_dim(block, block.shape[dim] - width, None, axis...  28.6 us
    ppermute x8, waiting for transfers between devices, with_halo(): lax.ppermute(lax.slice_in_dim(block, 0, width, axis=dim), axis, backward)  22.5 us
    ppermute x4, waiting for transfers between devices, from_behind(): return lax.ppermute(array, axis, pairs)  19.6 us
    ppermute x4, starting transfers between devices, from_behind(): return lax.ppermute(array, axis, pairs)  12.9 us
    ppermute x8, starting transfers between devices, with_halo(): lax.ppermute(lax.slice_in_dim(block, 0, width, axis=dim), axis, backward)  10.3 us
  transfers between devices with their start and end apart: 21, of which 10 were waited for; matrix products, arithmetic and copies ran while one was open for 6% of the time, Pallas kernels for 0%

commit v1 on v0

v1 whole, which is shorter than its diff:
```python
import functools

import jax
import jax.numpy as jnp
from jax import lax
from jax.experimental import pallas as pl
from jax.experimental.pallas import tpu as pltpu
from jax.sharding import PartitionSpec as P

SWEEPS = 4
ITERS = 2
MESH = pl.DeviceIdType.MESH
F32 = jnp.float32
BF16 = jnp.bfloat16


def torus_offsets(nx, ny):
    offsets = [(dx, dy) for dy in range(ny) for dx in range(nx)]
    hops = lambda o: min(o[0], nx - o[0]) + min(o[1], ny - o[1])
    order = sorted(range(1, nx * ny), key=lambda i: -hops(offsets[i]))
    return offsets, order


def kernel(
    shape,
    pairs_s,
    owner_s,
    wave_s,
    absorb_s,
    design_s,
    pairs_h,
    fields_h,
    source_h,
    labels_h,
    blocks_h,
    forward_h,
    adjoint_h,
    pairs_v,
    own,
    beside,
    coef,
    labels,
    block,
    facing_in,
    jumps,
    stacked,
    outgoing,
    products,
    rows32,
    face,
    left_out,
    right_out,
    left_in,
    right_in,
    halo_out,
    halo_in,
    load_sem,
    trace_sem,
    jump_send,
    jump_recv,
    prod_send,
    prod_recv,
    ghost_send,
    ghost_recv,
    halo_send,
    halo_recv,
    store_sem,
):
    n_dom, n_sub, nx = shape
    ny = n_sub // nx
    layers = fields_h.shape[1]
    offsets, order = torus_offsets(nx, ny)
    me_d = lax.axis_index("dom")
    me_s = lax.axis_index("sub")
    my_x, my_y = lax.rem(me_s, nx), lax.div(me_s, nx)
    before_d, after_d = lax.rem(me_d + n_dom - 1, n_dom), lax.rem(me_d + 1, n_dom)
    before_s, after_s = lax.rem(me_s + n_sub - 1, n_sub), lax.rem(me_s + 1, n_sub)

    def member(slot):
        dx, dy = offsets[slot]
        return lax.rem(my_y + dy, ny) * nx + lax.rem(my_x + dx, nx)

    loads = [
        pltpu.make_async_copy(pairs_h, pairs_v, load_sem.at[0]),
        pltpu.make_async_copy(fields_h, own.at[0], load_sem.at[1]),
        pltpu.make_async_copy(labels_h, labels, load_sem.at[2]),
        pltpu.make_async_copy(source_h, coef.at[2:4, 0], load_sem.at[3]),
        pltpu.make_async_copy(blocks_h.at[0, 0], block, load_sem.at[4]),
    ]
    for load in loads:
        load.start()

    barrier = pltpu.get_barrier_semaphore()
    greeted = [(me_d, member(slot)) for slot in order]
    for dom in (before_d, after_d):
        for sub in (before_s, me_s, after_s):
            greeted.append((dom, sub))
    for device in greeted:
        pl.semaphore_signal(barrier, inc=1, device_id=device, device_id_type=MESH)

    row = lax.broadcasted_iota(jnp.int32, (8, 128), 0)
    lane = lax.broadcasted_iota(jnp.int32, (8, 128), 1)
    upper = row < 4
    even = lax.rem(row, 2) == 0
    not_first = jnp.where(me_d == 0, 0.0, 1.0).astype(F32)
    not_last = jnp.where(me_d == n_dom - 1, 0.0, 1.0).astype(F32)
    has_before = jnp.where(me_s == 0, 0.0, 1.0).astype(F32)
    has_after = jnp.where(me_s == n_sub - 1, 0.0, 1.0).astype(F32)
    beside_mask = jnp.where(upper, has_after, has_before)

    def roll4(value):
        return pltpu.roll(value, 4, 0)

    wave = jnp.zeros((8, 128), F32)
    absorb = jnp.zeros((8, 128), F32)
    weight_table = jnp.zeros((8, 128), F32)
    for m in range(16):
        wave = jnp.where(lane == m, wave_s[m], wave)
        absorb = jnp.where(lane == m, absorb_s[m], absorb)
        weight_table = jnp.where(lane == m, design_s[m], weight_table)
    shifted = 6.0 - wave
    modulus = shifted * shifted + absorb * absorb
    real_table = shifted / modulus
    imag_table = absorb / modulus

    def look(table, index):
        return jnp.take_along_axis(table, index, axis=1, mode="promise_in_bounds")

    position = row * 128 + lane

    def place(step, carry):
        for t in range(16):
            point = step * 16 + t
            carry = jnp.where(position == pairs_s[0, point], point, carry)
        return carry

    inverse = lax.fori_loop(0, 64, place, jnp.zeros((8, 128), jnp.int32))
    loads[0].wait()
    pairs = pairs_v[...]

    def gather_points(read_row, index):
        index_row = lax.shift_right_logical(index, 7)
        index_lane = lax.bitwise_and(index, 127)
        out = jnp.zeros((8, 128), F32)
        for r in range(8):
            source_row = jnp.broadcast_to(read_row(r), (8, 128))
            out = jnp.where(index_row == r, look(source_row, index_lane), out)
        return out

    pl.semaphore_wait(barrier, len(greeted))

    def trace_copy(it):
        return pltpu.make_async_remote_copy(
            src_ref=fields_h.at[:, 0] if it == 0 else own.at[0, :, 0],
            dst_ref=facing_in.at[it],
            send_sem=trace_sem.at[0, it],
            recv_sem=trace_sem.at[1, it],
            device_id=(before_d, me_s),
            device_id_type=MESH,
        )

    def jump_copy(it, slot):
        return pltpu.make_async_remote_copy(
            src_ref=jumps.at[it, 0],
            dst_ref=jumps.at[it, slot],
            send_sem=jump_send.at[it, slot],
            recv_sem=jump_recv.at[it, slot],
            device_id=(me_d, member(slot)),
            device_id_type=MESH,
        )

    def product_copy(it, slot):
        dx, dy = offsets[slot]
        back = lax.rem(my_y + ny - dy, ny) * nx + lax.rem(my_x + nx - dx, nx)
        return pltpu.make_async_remote_copy(
            src_ref=outgoing.at[it, slot],
            dst_ref=products.at[it, slot],
            send_sem=prod_send.at[it, slot],
            recv_sem=prod_recv.at[it, slot],
            device_id=(me_d, back),
            device_id_type=MESH,
        )

    def ghost_copies(it):
        copies = []
        for k, (src, dst, device) in enumerate(
            (
                (left_out, left_in.at[it, 0], (after_d, me_s)),
                (left_out, left_in.at[it, 1], (after_d, after_s)),
                (left_out, left_in.at[it, 2], (after_d, before_s)),
                (right_out, right_in.at[it, 0], (me_d, after_s)),
                (right_out, right_in.at[it, 1], (me_d, before_s)),
            )
        ):
            copies.append(
                pltpu.make_async_remote_copy(
                    src_ref=src.at[it],
                    dst_ref=dst,
                    send_sem=ghost_send.at[it, k],
                    recv_sem=ghost_recv.at[it, k],
                    device_id=device,
                    device_id_type=MESH,
                )
            )
        return copies

    def halo_copies(it):
        count = halo_out.shape[1] if it == 0 else 4
        copies = []
        for k, sub in enumerate((after_s, before_s)):
            copies.append(
                pltpu.make_async_remote_copy(
                    src_ref=halo_out.at[k, 0:count] if it == 0 else halo_out.at[k + 2, 0:count],
                    dst_ref=halo_in.at[k, 0:count] if it == 0 else halo_in.at[k + 2, 0:count],
                    send_sem=halo_send.at[it, k],
                    recv_sem=halo_recv.at[it, k],
                    device_id=(me_d, sub),
                    device_id_type=MESH,
                )
            )
        return copies

    half = layers // 2

    def pack_halo(it, item, read):
        base = 2 * it

        def step(k, carry):
            downs, ups = [], []
            for t in range(2):
                near = read(2 * k + t)
                far = roll4(read(half + 2 * k + t))
                downs.append(jnp.where(upper, far, near))
                ups.append(jnp.where(upper, near, far))
            halo_out[base, item, k] = jnp.concatenate(downs, 0).astype(BF16)
            halo_out[base + 1, item, k] = jnp.concatenate(ups, 0).astype(BF16)
            return carry

        lax.fori_loop(0, half // 2, step, 0, unroll=4)

    def unpack_halo(it, item, write):
        base = 2 * it

        def step(k, carry):
            down = halo_in[base, item, k].astype(F32)
            up = halo_in[base + 1, item, k].astype(F32)
            for t in range(2):
                d, u = down[8 * t : 8 * t + 8], up[8 * t : 8 * t + 8]
                write(2 * k + t, jnp.where(upper, u, d))
                write(half + 2 * k + t, roll4(jnp.where(upper, d, u)))
            return carry

        lax.fori_loop(0, half // 2, step, 0, unroll=2)

    def z_sum(v):
        low = jnp.where(lane == 0, 0.0, pltpu.roll(v, 1, 1))
        high = jnp.where(lane == 127, 0.0, pltpu.roll(v, 127, 1))
        return low + high

    def relax(cur, across, layer, tiles):
        sums = [[None] * 4 for _ in range(2)]
        for c in range(4):
            a, b = cur[0][c], cur[1][c]
            a_up, b_up = pltpu.roll(a, 1, 0), pltpu.roll(b, 1, 0)
            a_dn, b_dn = pltpu.roll(a, 7, 0), pltpu.roll(b, 7, 0)
            for t in tiles:
                v = (a, b)[t]
                mine_up, mine_dn = ((a_up, a_dn), (b_up, b_dn))[t]
                other_up, other_dn = ((b_up, b_dn), (a_up, a_dn))[t]
                y_sum = jnp.where(row == 0, other_up, mine_up) + jnp.where(
                    row == 7, other_dn, mine_dn
                )
                sums[t][c] = across[t][c] + y_sum + z_sum(v)
        results = []
        for t in tiles:
            rr, ri = coef[0, t, layer], coef[1, t, layer]
            w = coef[4, t, layer]
            fr = coef[2, t, layer] + sums[t][0]
            fi = coef[3, t, layer] + sums[t][1]
            ar = w * cur[t][0] + sums[t][2]
            ai = w * cur[t][1] + sums[t][3]
            results.append(
                (rr * fr - ri * fi, rr * fi + ri * fr, rr * ar + ri * ai, rr * ai - ri * ar)
            )
        return results

    buffers = (own, beside)

    def sweep_run(level, first, count, tiles):
        src, dst = level % 2, (level + 1) % 2

        def fetch(layer):
            return [[buffers[t][src, c, layer] for c in range(4)] for t in range(2)]

        values = [fetch(first + i) for i in range(-1, count + 1)]
        for i in range(count):
            low, cur, high = values[i], values[i + 1], values[i + 2]
            across = [[low[t][c] + high[t][c] for c in range(4)] for t in range(2)]
            results = relax(cur, across, first + i, tiles)
            for t, result in zip(tiles, results):
                for c in range(4):
                    buffers[t][dst, c, first + i] = result[c]

    def sweep_inside(level):
        tiles = (0, 1) if level < SWEEPS - 1 else (0,)
        first, last = level + 1, layers - 2 - level
        total = last - first + 1
        chunk = 4
        trips = total // chunk

        def step(k, carry):
            sweep_run(level, first + k * chunk, chunk, tiles)
            return carry

        lax.fori_loop(0, trips, step, 0)
        if total - trips * chunk:
            sweep_run(level, first + trips * chunk, total - trips * chunk, tiles)

    def sweep_end(level, ghosts, at_start):
        tiles = (0, 1) if level < SWEEPS - 1 else (0,)
        src, dst = level % 2, (level + 1) % 2
        count = level + 1
        span = range(0, count) if at_start else range(layers - count, layers)

        def fetch(layer):
            if layer < 0 or layer >= layers:
                return ghosts
            return [[buffers[t][src, c, layer] for c in range(4)] for t in range(2)]

        values = {layer: fetch(layer) for layer in range(span[0] - 1, span[-1] + 2)}
        for layer in span:
            low, cur, high = values[layer - 1], values[layer], values[layer + 1]
            across = [[low[t][c] + high[t][c] for c in range(4)] for t in range(2)]
            results = relax(cur, across, layer, tiles)
            for t, result in zip(tiles, results):
                for c in range(4):
                    buffers[t][dst, c, layer] = result[c]

    def coefficients_of(tile, mask=None, read=None):
        def step(layer, carry):
            lab = read(layer)
            rr, ri = look(real_table, lab), look(imag_table, lab)
            if mask is not None:
                rr, ri = rr * mask, ri * mask
            coef[0, tile, layer] = rr
            coef[1, tile, layer] = ri
            coef[4, tile, layer] = look(weight_table, lab)
            return carry

        lax.fori_loop(0, layers, step, 0, unroll=4)

    trace_copy(0).start()
    loads[1].wait()
    loads[2].wait()
    loads[3].wait()

    for it in range(ITERS):
        trace = trace_copy(it)
        if it == 0:
            pack_halo(0, 0, lambda l: own[0, 0, l])
            pack_halo(0, 1, lambda l: own[0, 1, l])
        trace.wait_recv()
        facing = []
        for c in range(4):
            taken = gather_points(lambda r: facing_in[it, c, r : r + 1, :], pairs)
            taken = taken * not_last
            facing.append(taken)
            face[c] = taken
            rows32[pl.ds(c, 8, stride=4), :] = taken - own[0, c, layers - 1]
        jumps[it, 0] = rows32[...].astype(BF16)
        for slot in order:
            jump_copy(it, slot).start()

        first_item = 2 if it == 0 else 0
        for c in range(first_item, 4):
            pack_halo(it, c, lambda l, c=c: own[0, c, l])
        if it == 0:
            pack_halo(0, 4, lambda l: coef[2, 0, l])
            pack_halo(0, 5, lambda l: coef[3, 0, l])
            pack_halo(0, 6, lambda l: labels[l].astype(F32))
        for copy in halo_copies(it):
            copy.start()
        if it == 0:
            coefficients_of(0, read=lambda l: labels[l])
            loads[4].wait()

        for slot in order:
            jump_copy(it, slot).wait_recv()
        for i in range(0, n_sub, 4):
            first = [jumps[it, i + t].astype(F32) for t in range(4)]
            for r in range(8):
                k, odd = r // 2, r % 2
                plain, turned = [], []
                for t in (0, 2):
                    a = first[t][8 * k : 8 * k + 8]
                    b = first[t + 1][8 * k : 8 * k + 8]
                    v = jnp.where(upper, roll4(a) if odd else a, b if odd else roll4(b))
                    plain.append(v)
                    turned.append(jnp.where(even, -pltpu.roll(v, 7, 0), pltpu.roll(v, 1, 0)))
                stacked[0, 4 * i : 4 * i + 16, r * 128 : r * 128 + 128] = jnp.concatenate(
                    plain, 0
                ).astype(BF16)
                stacked[1, 4 * i : 4 * i + 16, r * 128 : r * 128 + 128] = jnp.concatenate(
                    turned, 0
                ).astype(BF16)
        contract = (((1,), (1,)), ((), ()))
        total = lax.dot_general(
            stacked[0], block[0], contract, preferred_element_type=F32
        ) + lax.dot_general(stacked[1], block[1], contract, preferred_element_type=F32)
        for i in range(0, n_sub, 2):
            rows = total[4 * i : 4 * i + 8]
            evens, odds = [], []
            for k in range(4):
                a = rows[:, 256 * k : 256 * k + 128]
                b = rows[:, 256 * k + 128 : 256 * k + 256]
                evens.append(jnp.where(upper, a, roll4(b)))
                odds.append(jnp.where(upper, roll4(a), b))
            outgoing[it, i] = jnp.concatenate(evens, 0).astype(BF16)
            outgoing[it, i + 1] = jnp.concatenate(odds, 0).astype(BF16)
        for slot in order:
            product_copy(it, slot).start()
        products[it, 0] = outgoing[it, 0]

        for copy in halo_copies(it):
            copy.wait_recv()
        for c in range(4):
            def write_field(l, v, c=c):
                beside[0, c, l] = v * beside_mask

            unpack_halo(it, c, write_field)
        if it == 0:
            for c in range(2):
                def write_source(l, v, c=c):
                    coef[2 + c, 1, l] = v

                unpack_halo(0, 4 + c, write_source)

            def write_coef(l, v):
                lab = v.astype(jnp.int32)
                coef[0, 1, l] = look(real_table, lab) * beside_mask
                coef[1, 1, l] = look(imag_table, lab) * beside_mask
                coef[4, 1, l] = look(weight_table, lab)

            unpack_halo(0, 6, write_coef)
        for level in range(SWEEPS):
            sweep_inside(level)

        for slot in order:
            product_copy(it, slot).wait_recv()
        owner = owner_s[0, me_s]
        owner_dx = lax.rem(lax.rem(owner, nx) - my_x + nx, nx)
        owner_dy = lax.rem(lax.div(owner, nx) - my_y + ny, ny)
        rows32[...] = products[it, owner_dy * nx + owner_dx].astype(F32)
        right_own, back = [], []
        for c in range(4):
            moved = rows32[pl.ds(c, 8, stride=4), :]
            right = (face[c] + moved) * not_last
            right_own.append(right)
            right_out[it, c] = right
            face[c] = own[0, c, layers - 1] - moved
        for c in range(4):
            left_out[it, c] = gather_points(lambda r: face[c, r : r + 1, :], inverse)
        ghosts = ghost_copies(it)
        for copy in ghosts:
            copy.start()
        trace.wait_send()
        for copy in ghosts[3:]:
            copy.wait_recv()
        right_ghosts = [
            right_own,
            [jnp.where(upper, right_in[it, 1, c], right_in[it, 0, c]) for c in range(4)],
        ]
        for level in range(SWEEPS):
            sweep_end(level, right_ghosts, False)
        for copy in ghosts[:3]:
            copy.wait_recv()
        left_ghosts = [
            [left_in[it, 0, c] * not_first for c in range(4)],
            [
                jnp.where(upper, left_in[it, 2, c], left_in[it, 1, c]) * not_first
                for c in range(4)
            ],
        ]
        for level in range(SWEEPS):
            sweep_end(level, left_ghosts, True)
        if it + 1 < ITERS:
            trace_copy(it + 1).start()
        for slot in order:
            jump_copy(it, slot).wait_send()
            product_copy(it, slot).wait_send()
        for copy in ghosts + halo_copies(it):
            copy.wait_send()

    stores = [
        pltpu.make_async_copy(own.at[0, 0:2], forward_h, store_sem.at[0]),
        pltpu.make_async_copy(own.at[0, 2:4], adjoint_h, store_sem.at[1]),
    ]
    for store in stores:
        store.start()
    for store in stores:
        store.wait()


def solution(mesh):
    n_dom, n_sub = mesh.shape["dom"], mesh.shape["sub"]
    nx = 4 if n_sub % 4 == 0 and n_sub > 4 else 2

    def per_device(
        start_fields,
        source,
        labels,
        wavenumber2,
        absorption,
        design_weight,
        pairs,
        block_index,
        blocks,
    ):
        layers = labels.shape[0]
        points = pairs.shape[-1]
        slots = n_sub
        smem = pl.BlockSpec(memory_space=pltpu.SMEM)
        hbm = pl.BlockSpec(memory_space=pl.ANY)
        out = jax.ShapeDtypeStruct((2,) + labels.shape, F32)
        dma = pltpu.SemaphoreType.DMA
        return pl.pallas_call(
            functools.partial(kernel, (n_dom, n_sub, nx)),
            out_shape=(out, out),
            in_specs=[smem] * 5 + [hbm] * 5,
            out_specs=(hbm, hbm),
            scratch_shapes=[
                pltpu.VMEM((8, 128), jnp.int32),
                pltpu.VMEM((2, 4, layers, 8, 128), F32),
                pltpu.VMEM((2, 4, layers, 8, 128), F32),
                pltpu.VMEM((5, 2, layers, 8, 128), F32),
                pltpu.VMEM((layers, 8, 128), jnp.int32),
                pltpu.VMEM((2, points, points), BF16),
                pltpu.VMEM((ITERS, 4, 8, 128), F32),
                pltpu.VMEM((ITERS, slots, 32, 128), BF16),
                pltpu.VMEM((2, 4 * slots, points), BF16),
                pltpu.VMEM((ITERS, slots, 32, 128), BF16),
                pltpu.VMEM((ITERS, slots, 32, 128), BF16),
                pltpu.VMEM((32, 128), F32),
                pltpu.VMEM((4, 8, 128), F32),
                pltpu.VMEM((ITERS, 4, 8, 128), F32),
                pltpu.VMEM((ITERS, 4, 8, 128), F32),
                pltpu.VMEM((ITERS, 3, 4, 8, 128), F32),
                pltpu.VMEM((ITERS, 2, 4, 8, 128), F32),
                pltpu.VMEM((4, 7, layers // 4, 16, 128), BF16),
                pltpu.VMEM((4, 7, layers // 4, 16, 128), BF16),
                dma((5,)),
                dma((2, ITERS)),
                dma((ITERS, slots)),
                dma((ITERS, slots)),
                dma((ITERS, slots)),
                dma((ITERS, slots)),
                dma((ITERS, 5)),
                dma((ITERS, 5)),
                dma((ITERS, 2)),
                dma((ITERS, 2)),
                dma((2,)),
            ],
            compiler_params=pltpu.CompilerParams(
                collective_id=0, has_side_effects=True, vmem_limit_bytes=48 * 1024 * 1024
            ),
        )(
            pairs[0],
            block_index,
            wavenumber2,
            absorption,
            design_weight,
            pairs.reshape(8, 128),
            start_fields,
            source,
            labels,
            blocks,
        )

    placed = (
        P(None, "dom", "sub", None),
        P(None, "dom", "sub", None),
        P("dom", "sub", None),
        P(),
        P(),
        P(),
        P("dom", "sub", None),
        P("dom", None),
        P("dom", "sub", None, None, None),
    )
    return jax.shard_map(
        per_device,
        mesh=mesh,
        in_specs=placed,
        out_specs=(P(None, "dom", "sub", None), P(None, "dom", "sub", None)),
        check_vma=False,
    )
```

time: 515 us -> 61.8 us (0.12); the launches traced: 507 us -> 60.9 us
  waiting for transfers between devices: 405 us -> 0 us
  starting transfers between devices: 51.8 us -> 0 us
  Pallas kernels: 0 us -> 50.5 us
  between operations: 15.4 us -> 0.66 us
  local copies, waits for them, and re-layouts: 19.9 us -> 9.79 us
  matrix products: 8.99 us -> 0 us
  other arithmetic: 6.14 us -> 0 us
    all_gather x1 -> x0, waiting for transfers between devices: 362 us -> none  [per_device(): library = lax.all_gather(blocks, 'sub', axis=1, tiled=True)]
    ppermute x20 -> x0, starting transfers between devices: 51.8 us -> none  [the longest x8 28.6 us: with_halo(): lax.ppermute(lax.slice_in_dim(block, block.shape[dim] - width, None, axis...]
    pallas_call x0 -> x1, Pallas kernels: none -> 50.5 us  [per_device(): pl.pallas_call(functools.partial(kernel, (n_dom, n_sub, nx)), out_shape=(...]
    ppermute x20 -> x0, waiting for transfers between devices: 42.2 us -> none  [the longest x8 22.5 us: with_halo(): lax.ppermute(lax.slice_in_dim(block, 0, width, axis=dim), axis, backward)]
    gather x6 -> x0, local copies, waits for them, and re-layouts: 12.7 us -> none  [the longest x4 7.03 us: per_device(): facing = jnp.take(following, facing_order, axis=1)]
    unnamed x20, local copies, waits for them, and re-layouts: 0.41 us -> 9.79 us
    dot_general x4 -> x0, matrix products: 8.99 us -> none  [the longest x2 4.51 us: products(): lax.dot_general(row_block, matrix_pair[1], contract, preferred_element_ty...]
  transfers between devices with their start and end apart: 21 -> 0, of which waited for: 10 -> 0; matrix products, arithmetic and copies ran while one was open for 6% -> 0% of each run, Pallas kernels for 0% -> 0%
where the time goes in v1:
time: 61.8 us; the launch traced here: 60.9 us
  Pallas kernels  50.5 us (82%)
  local copies, waits for them, and re-layouts  9.79 us (16%)
  between operations  0.66 us (1%)
    pallas_call x1, Pallas kernels, per_device(): pl.pallas_call(functools.partial(kernel, (n_dom, n_sub, nx)), out_shape=(...  50.5 us
    unnamed x20, local copies, waits for them, and re-layouts  9.79 us

profile of v1, /device:TPU:1, one launch (start us, length us, event | category | flops | bytes accessed | tf_op | source)
XLA Modules:
  0.0 60.9 jit_solution(6399146400723315559)
XLA Ops:
  0.6 0.0 copy-start
  0.6 2.2 %copy-done = bf16[1,1,2,1024,1024]{4,3,2,1,0:T(8,128)(2,1)S(1)} copy-done((bf16[1,1,2,1024,1024]{4,3,2,1,0:T(8,128)(2,1)S(1)}, bf16[1,1,2,1024,1024]{4,3,2,1,0:T(8,128)(2,1)}, u32[]{:S(2)}) %copy-start) | copy-done | bytes 4194328
  2.8 0.0 copy-start.1
  2.8 1.0 %copy-done.1 = f32[4,32,8,128]{3,2,1,0:T(8,128)S(1)} copy-done((f32[4,32,8,128]{3,2,1,0:T(8,128)S(1)}, f32[4,32,8,128]{3,2,1,0:T(8,128)}, u32[]{:S(2)}) %copy-start.1) | copy-done | bytes 524312
  3.9 0.0 copy-start.2
  3.9 0.9 %copy-done.2 = f32[2,32,8,128]{3,2,1,0:T(8,128)S(1)} copy-done((f32[2,32,8,128]{3,2,1,0:T(8,128)S(1)}, f32[2,32,8,128]{3,2,1,0:T(8,128)}, u32[]{:S(2)}) %copy-start.2) | copy-done | bytes 262168
  4.8 0.0 copy-start.3
  4.8 0.9 %copy-done.3 = s32[32,8,128]{2,1,0:T(8,128)S(1)} copy-done((s32[32,8,128]{2,1,0:T(8,128)S(1)}, s32[32,8,128]{2,1,0:T(8,128)}, u32[]{:S(2)}) %copy-start.3) | copy-done | bytes 131096
  5.7 0.0 copy-start.4
  5.7 0.7 %copy-done.4 = s32[1,1,1024]{2,1,0:T(1,128)S(1)} copy-done((s32[1,1,1024]{2,1,0:T(1,128)S(1)}, s32[1,1,1024]{2,1,0:T(1,128)}, u32[]{:S(2)}) %copy-start.4) | copy-done | bytes 4120
  6.4 0.0 copy-start.5
  6.4 0.7 %copy-done.5 = s32[1,16]{1,0:T(1,128)S(1)} copy-done((s32[1,16]{1,0:T(1,128)S(1)}, s32[1,16]{1,0:T(1,128)}, u32[]{:S(2)}) %copy-start.5) | copy-done | bytes 88
  7.1 0.0 copy-start.6
  7.1 0.7 %copy-done.6 = f32[16]{0:T(128)S(1)} copy-done((f32[16]{0:T(128)S(1)}, f32[16]{0:T(128)}, u32[]{:S(2)}) %copy-start.6) | copy-done | bytes 88
  7.7 0.0 copy-start.7
  7.7 0.7 %copy-done.7 = f32[16]{0:T(128)S(1)} copy-done((f32[16]{0:T(128)S(1)}, f32[16]{0:T(128)}, u32[]{:S(2)}) %copy-start.7) | copy-done | bytes 88
  8.4 0.0 copy-start.8
  8.4 0.7 %copy-done.8 = f32[16]{0:T(128)S(1)} copy-done((f32[16]{0:T(128)S(1)}, f32[16]{0:T(128)}, u32[]{:S(2)}) %copy-start.8) | copy-done | bytes 88
  9.0 50.5 %shard_map.104 = (f32[2,32,8,128]{3,2,1,0:T(8,128)S(1)}, f32[2,32,8,128]{3,2,1,0:T(8,128)S(1)}) custom-call(s32[1,1024]{1,0:T(1,128)S(1)} %bitcast.2, s32[1,16]{1,0:T(1,128)S(1)} %copy-done.5, f32[16]{0:T(128)S(1)} %copy-done.6, f32[16]{0:T(128)S(1)} %copy-done.7, f32[16]{0:T(128)S(1)} %copy-done.8, s32[8,128]{1,0:T(8,128)S(1)} %bitcast.3, ...), custom_call_target="tpu_custom_call" | custom-call | tf_op jit(solution)/shard_map/pallas_call | solution.py:526
  59.5 0.7 %copy.13 = f32[2,32,8,128]{3,2,1,0:T(8,128)} copy(f32[2,32,8,128]{3,2,1,0:T(8,128)S(1)} %get-tuple-element.4) | data formatting | bytes 524288
  60.2 0.7 %copy.14 = f32[2,32,8,128]{3,2,1,0:T(8,128)} copy(f32[2,32,8,128]{3,2,1,0:T(8,128)S(1)} %get-tuple-element.5) | data formatting | bytes 524288
Async XLA Ops:
  0.6 2.2 %copy-start = (bf16[1,1,2,1024,1024]{4,3,2,1,0:T(8,128)(2,1)S(1)}, bf16[1,1,2,1024,1024]{4,3,2,1,0:T(8,128)(2,1)}, u32[]{:S(2)}) copy-start(bf16[1,1,2,1024,1024]{4,3,2,1,0:T(8,128)(2,1)} %blocks_h.1) | copy-start | bytes 12582916
  2.8 1.0 %copy-start.1 = (f32[4,32,8,128]{3,2,1,0:T(8,128)S(1)}, f32[4,32,8,128]{3,2,1,0:T(8,128)}, u32[]{:S(2)}) copy-start(f32[4,32,8,128]{3,2,1,0:T(8,128)} %fields_h.1) | copy-start | bytes 1572868
  3.9 0.9 %copy-start.2 = (f32[2,32,8,128]{3,2,1,0:T(8,128)S(1)}, f32[2,32,8,128]{3,2,1,0:T(8,128)}, u32[]{:S(2)}) copy-start(f32[2,32,8,128]{3,2,1,0:T(8,128)} %source_h.1) | copy-start | bytes 786436
  4.8 0.9 %copy-start.3 = (s32[32,8,128]{2,1,0:T(8,128)S(1)}, s32[32,8,128]{2,1,0:T(8,128)}, u32[]{:S(2)}) copy-start(s32[32,8,128]{2,1,0:T(8,128)} %labels_h.1) | copy-start | bytes 393220
  5.7 0.7 %copy-start.4 = (s32[1,1,1024]{2,1,0:T(1,128)S(1)}, s32[1,1,1024]{2,1,0:T(1,128)}, u32[]{:S(2)}) copy-start(s32[1,1,1024]{2,1,0:T(1,128)} %param.15) | copy-start | bytes 12292
  6.4 0.7 %copy-start.5 = (s32[1,16]{1,0:T(1,128)S(1)}, s32[1,16]{1,0:T(1,128)}, u32[]{:S(2)}) copy-start(s32[1,16]{1,0:T(1,128)} %owner_s.1) | copy-start | bytes 196
  7.1 0.7 %copy-start.6 = (f32[16]{0:T(128)S(1)}, f32[16]{0:T(128)}, u32[]{:S(2)}) copy-start(f32[16]{0:T(128)} %wave_s.1) | copy-start | bytes 196
  7.7 0.7 %copy-start.7 = (f32[16]{0:T(128)S(1)}, f32[16]{0:T(128)}, u32[]{:S(2)}) copy-start(f32[16]{0:T(128)} %absorb_s.1) | copy-start | bytes 196
  8.4 0.7 %copy-start.8 = (f32[16]{0:T(128)S(1)}, f32[16]{0:T(128)}, u32[]{:S(2)}) copy-start(f32[16]{0:T(128)} %design_s.1) | copy-start | bytes 196

commit v2 on v1

--- a/solution.py
+++ b/solution.py
@@ -23,18 +23,23 @@
 
 def kernel(
     shape,
+    pairs_flat_h,
+    owner_h,
+    wave_h,
+    absorb_h,
+    design_h,
+    pairs_h,
+    fields_h,
+    source_h,
+    labels_h,
+    blocks_h,
+    forward,
+    adjoint,
     pairs_s,
     owner_s,
     wave_s,
     absorb_s,
     design_s,
-    pairs_h,
-    fields_h,
-    source_h,
-    labels_h,
-    blocks_h,
-    forward_h,
-    adjoint_h,
     pairs_v,
     own,
     beside,
@@ -64,7 +69,6 @@
     ghost_recv,
     halo_send,
     halo_recv,
-    store_sem,
 ):
     n_dom, n_sub, nx = shape
     ny = n_sub // nx
@@ -80,6 +84,20 @@
         dx, dy = offsets[slot]
         return lax.rem(my_y + dy, ny) * nx + lax.rem(my_x + dx, nx)
 
+    small_loads = [
+        pltpu.make_async_copy(src, dst, load_sem.at[5 + k])
+        for k, (src, dst) in enumerate(
+            (
+                (pairs_flat_h, pairs_s),
+                (owner_h, owner_s),
+                (wave_h, wave_s),
+                (absorb_h, absorb_s),
+                (design_h, design_s),
+            )
+        )
+    ]
+    for load in small_loads:
+        load.start()
     loads = [
         pltpu.make_async_copy(pairs_h, pairs_v, load_sem.at[0]),
         pltpu.make_async_copy(fields_h, own.at[0], load_sem.at[1]),
@@ -87,7 +105,7 @@
         pltpu.make_async_copy(source_h, coef.at[2:4, 0], load_sem.at[3]),
         pltpu.make_async_copy(blocks_h.at[0, 0], block, load_sem.at[4]),
     ]
-    for load in loads:
+    for load in loads[:4]:
         load.start()
 
     barrier = pltpu.get_barrier_semaphore()
@@ -111,44 +129,6 @@
     def roll4(value):
         return pltpu.roll(value, 4, 0)
 
-    wave = jnp.zeros((8, 128), F32)
-    absorb = jnp.zeros((8, 128), F32)
-    weight_table = jnp.zeros((8, 128), F32)
-    for m in range(16):
-        wave = jnp.where(lane == m, wave_s[m], wave)
-        absorb = jnp.where(lane == m, absorb_s[m], absorb)
-        weight_table = jnp.where(lane == m, design_s[m], weight_table)
-    shifted = 6.0 - wave
-    modulus = shifted * shifted + absorb * absorb
-    real_table = shifted / modulus
-    imag_table = absorb / modulus
-
-    def look(table, index):
-        return jnp.take_along_axis(table, index, axis=1, mode="promise_in_bounds")
-
-    position = row * 128 + lane
-
-    def place(step, carry):
-        for t in range(16):
-            point = step * 16 + t
-            carry = jnp.where(position == pairs_s[0, point], point, carry)
-        return carry
-
-    inverse = lax.fori_loop(0, 64, place, jnp.zeros((8, 128), jnp.int32))
-    loads[0].wait()
-    pairs = pairs_v[...]
-
-    def gather_points(read_row, index):
-        index_row = lax.shift_right_logical(index, 7)
-        index_lane = lax.bitwise_and(index, 127)
-        out = jnp.zeros((8, 128), F32)
-        for r in range(8):
-            source_row = jnp.broadcast_to(read_row(r), (8, 128))
-            out = jnp.where(index_row == r, look(source_row, index_lane), out)
-        return out
-
-    pl.semaphore_wait(barrier, len(greeted))
-
     def trace_copy(it):
         return pltpu.make_async_remote_copy(
             src_ref=fields_h.at[:, 0] if it == 0 else own.at[0, :, 0],
@@ -169,14 +149,15 @@
             device_id_type=MESH,
         )
 
-    def product_copy(it, slot):
+    def product_copy(it, slot, part):
         dx, dy = offsets[slot]
         back = lax.rem(my_y + ny - dy, ny) * nx + lax.rem(my_x + nx - dx, nx)
+        rows = pl.ds(16 * part, 16)
         return pltpu.make_async_remote_copy(
-            src_ref=outgoing.at[it, slot],
-            dst_ref=products.at[it, slot],
-            send_sem=prod_send.at[it, slot],
-            recv_sem=prod_recv.at[it, slot],
+            src_ref=outgoing.at[it, slot, rows],
+            dst_ref=products.at[it, slot, rows],
+            send_sem=prod_send.at[it, slot, part],
+            recv_sem=prod_recv.at[it, slot, part],
             device_id=(me_d, back),
             device_id_type=MESH,
         )
@@ -204,16 +185,21 @@
             )
         return copies
 
-    def halo_copies(it):
-        count = halo_out.shape[1] if it == 0 else 4
+    def halo_copies(it, second=False):
+        groups = halo_out.shape[2]
+        if it == 0:
+            items, span = ((4, 3) if second else (0, 4)), (0, groups)
+        else:
+            items, span = (0, 4), ((0, 2) if second else (2, groups - 2))
         copies = []
         for k, sub in enumerate((after_s, before_s)):
+            part = (2 * it + k, pl.ds(*items), pl.ds(*span))
             copies.append(
                 pltpu.make_async_remote_copy(
-                    src_ref=halo_out.at[k, 0:count] if it == 0 else halo_out.at[k + 2, 0:count],
-                    dst_ref=halo_in.at[k, 0:count] if it == 0 else halo_in.at[k + 2, 0:count],
-                    send_sem=halo_send.at[it, k],
-                    recv_sem=halo_recv.at[it, k],
+                    src_ref=halo_out.at[part],
+                    dst_ref=halo_in.at[part],
+                    send_sem=halo_send.at[2 * it + second, k],
+                    recv_sem=halo_recv.at[2 * it + second, k],
                     device_id=(me_d, sub),
                     device_id_type=MESH,
                 )
@@ -222,23 +208,23 @@
 
     half = layers // 2
 
-    def pack_halo(it, item, read):
+    def pack_halo(it, item, read, start=0, stop=None):
         base = 2 * it
 
         def step(k, carry):
             downs, ups = [], []
             for t in range(2):
                 near = read(2 * k + t)
-                far = roll4(read(half + 2 * k + t))
+                far = roll4(read(layers - 1 - 2 * k - t))
                 downs.append(jnp.where(upper, far, near))
                 ups.append(jnp.where(upper, near, far))
             halo_out[base, item, k] = jnp.concatenate(downs, 0).astype(BF16)
             halo_out[base + 1, item, k] = jnp.concatenate(ups, 0).astype(BF16)
             return carry
 
-        lax.fori_loop(0, half // 2, step, 0, unroll=4)
-
-    def unpack_halo(it, item, write):
+        lax.fori_loop(start, stop or half // 2, step, 0, unroll=2)
+
+    def unpack_halo(it, item, write, start=0, stop=None):
         base = 2 * it
 
         def step(k, carry):
@@ -247,10 +233,17 @@
             for t in range(2):
                 d, u = down[8 * t : 8 * t + 8], up[8 * t : 8 * t + 8]
                 write(2 * k + t, jnp.where(upper, u, d))
-                write(half + 2 * k + t, roll4(jnp.where(upper, d, u)))
+                write(layers - 1 - 2 * k - t, roll4(jnp.where(upper, d, u)))
             return carry
 
-        lax.fori_loop(0, half // 2, step, 0, unroll=2)
+        lax.fori_loop(start, stop or half // 2, step, 0, unroll=2)
+
+    def unpack_fields(it, start, stop):
+        for c in range(4):
+            def write_field(l, v, c=c):
+                beside[0, c, l] = v * beside_mask
+
+            unpack_halo(it, c, write_field, start, stop)
 
     def z_sum(v):
         low = jnp.where(lane == 0, 0.0, pltpu.roll(v, 1, 1))
@@ -286,8 +279,14 @@
 
     buffers = (own, beside)
 
-    def sweep_run(level, first, count, tiles):
-        src, dst = level % 2, (level + 1) % 2
+    def put(level, final, t, c, layer, value):
+        if final and level == SWEEPS - 1:
+            (forward, adjoint)[c // 2][c % 2, layer] = value
+        else:
+            buffers[t][(level + 1) % 2, c, layer] = value
+
+    def sweep_run(level, first, count, tiles, final):
+        src = level % 2
 
         def fetch(layer):
             return [[buffers[t][src, c, layer] for c in range(4)] for t in range(2)]
@@ -299,26 +298,24 @@
             results = relax(cur, across, first + i, tiles)
             for t, result in zip(tiles, results):
                 for c in range(4):
-                    buffers[t][dst, c, first + i] = result[c]
-
-    def sweep_inside(level):
+                    put(level, final, t, c, first + i, result[c])
+
+    def sweep_inside(level, final):
         tiles = (0, 1) if level < SWEEPS - 1 else (0,)
         first, last = level + 1, layers - 2 - level
         total = last - first + 1
-        chunk = 4
-        trips = total // chunk
+        trips = 2
+        chunk = total // trips
 
         def step(k, carry):
-            sweep_run(level, first + k * chunk, chunk, tiles)
+            sweep_run(level, first + k * chunk, chunk, tiles, final)
             return carry
 
         lax.fori_loop(0, trips, step, 0)
-        if total - trips * chunk:
-            sweep_run(level, first + trips * chunk, total - trips * chunk, tiles)
-
-    def sweep_end(level, ghosts, at_start):
+
+    def sweep_end(level, ghosts, at_start, final):
         tiles = (0, 1) if level < SWEEPS - 1 else (0,)
-        src, dst = level % 2, (level + 1) % 2
+        src = level % 2
         count = level + 1
         span = range(0, count) if at_start else range(layers - count, layers)
 
@@ -334,7 +331,7 @@
             results = relax(cur, across, layer, tiles)
             for t, result in zip(tiles, results):
                 for c in range(4):
-                    buffers[t][dst, c, layer] = result[c]
+                    put(level, final, t, c, layer, result[c])
 
     def coefficients_of(tile, mask=None, read=None):
         def step(layer, carry):
@@ -349,16 +346,58 @@
 
         lax.fori_loop(0, layers, step, 0, unroll=4)
 
+    pl.semaphore_wait(barrier, len(greeted))
     trace_copy(0).start()
-    loads[1].wait()
-    loads[2].wait()
-    loads[3].wait()
+    for load in loads[1:4]:
+        load.wait()
+    loads[4].start()
+    pack_halo(0, 4, lambda l: coef[2, 0, l])
+    pack_halo(0, 5, lambda l: coef[3, 0, l])
+    pack_halo(0, 6, lambda l: labels[l].astype(F32))
+    for copy in halo_copies(0, True):
+        copy.start()
+    for c in range(4):
+        pack_halo(0, c, lambda l, c=c: own[0, c, l])
+    for load in small_loads:
+        load.wait()
+
+    wave = jnp.zeros((8, 128), F32)
+    absorb = jnp.zeros((8, 128), F32)
+    weight_table = jnp.zeros((8, 128), F32)
+    for m in range(16):
+        wave = jnp.where(lane == m, wave_s[m], wave)
+        absorb = jnp.where(lane == m, absorb_s[m], absorb)
+        weight_table = jnp.where(lane == m, design_s[m], weight_table)
+    shifted = 6.0 - wave
+    modulus = shifted * shifted + absorb * absorb
+    real_table = shifted / modulus
+    imag_table = absorb / modulus
+
+    def look(table, index):
+        return jnp.take_along_axis(table, index, axis=1, mode="promise_in_bounds")
+
+    position = row * 128 + lane
+
+    def place(step, carry):
+        for t in range(16):
+            point = step * 16 + t
+            carry = jnp.where(position == pairs_s[0, point], point, carry)
+        return carry
+
+    loads[0].wait()
+    pairs = pairs_v[...]
+
+    def gather_points(read_row, index):
+        index_row = lax.shift_right_logical(index, 7)
+        index_lane = lax.bitwise_and(index, 127)
+        out = jnp.zeros((8, 128), F32)
+        for r in range(8):
+            source_row = jnp.broadcast_to(read_row(r), (8, 128))
+            out = jnp.where(index_row == r, look(source_row, index_lane), out)
+        return out
 
     for it in range(ITERS):
         trace = trace_copy(it)
-        if it == 0:
-            pack_halo(0, 0, lambda l: own[0, 0, l])
-            pack_halo(0, 1, lambda l: own[0, 1, l])
         trace.wait_recv()
         facing = []
         for c in range(4):
@@ -371,19 +410,20 @@
         for slot in order:
             jump_copy(it, slot).start()
 
-        first_item = 2 if it == 0 else 0
-        for c in range(first_item, 4):
-            pack_halo(it, c, lambda l, c=c: own[0, c, l])
         if it == 0:
-            pack_halo(0, 4, lambda l: coef[2, 0, l])
-            pack_halo(0, 5, lambda l: coef[3, 0, l])
-            pack_halo(0, 6, lambda l: labels[l].astype(F32))
-        for copy in halo_copies(it):
-            copy.start()
-        if it == 0:
+            for copy in halo_copies(0):
+                copy.start()
             coefficients_of(0, read=lambda l: labels[l])
+            inverse = lax.fori_loop(0, 64, place, jnp.zeros((8, 128), jnp.int32))
             loads[4].wait()
-
+        else:
+            for c in range(4):
+                pack_halo(it, c, lambda l, c=c: own[0, c, l], 0, 2)
+            for copy in halo_copies(it, True):
+                copy.start()
+            for copy in halo_copies(it):
+                copy.wait_recv()
+            unpack_fields(it, 2, half // 2)
         for slot in order:
             jump_copy(it, slot).wait_recv()
         for i in range(0, n_sub, 4):
@@ -404,31 +444,33 @@
                     turned, 0
                 ).astype(BF16)
         contract = (((1,), (1,)), ((), ()))
-        total = lax.dot_general(
-            stacked[0], block[0], contract, preferred_element_type=F32
-        ) + lax.dot_general(stacked[1], block[1], contract, preferred_element_type=F32)
-        for i in range(0, n_sub, 2):
-            rows = total[4 * i : 4 * i + 8]
-            evens, odds = [], []
-            for k in range(4):
-                a = rows[:, 256 * k : 256 * k + 128]
-                b = rows[:, 256 * k + 128 : 256 * k + 256]
-                evens.append(jnp.where(upper, a, roll4(b)))
-                odds.append(jnp.where(upper, roll4(a), b))
-            outgoing[it, i] = jnp.concatenate(evens, 0).astype(BF16)
-            outgoing[it, i + 1] = jnp.concatenate(odds, 0).astype(BF16)
-        for slot in order:
-            product_copy(it, slot).start()
+        width = 512
+        for part in range(2):
+            span = pl.ds(width * part, width)
+            total = lax.dot_general(
+                stacked[0], block[0, span, :], contract, preferred_element_type=F32
+            ) + lax.dot_general(
+                stacked[1], block[1, span, :], contract, preferred_element_type=F32
+            )
+            for i in range(0, n_sub, 2):
+                rows = total[4 * i : 4 * i + 8]
+                evens, odds = [], []
+                for k in range(2):
+                    a = rows[:, 256 * k : 256 * k + 128]
+                    b = rows[:, 256 * k + 128 : 256 * k + 256]
+                    evens.append(jnp.where(upper, a, roll4(b)))
+                    odds.append(jnp.where(upper, roll4(a), b))
+                here = slice(16 * part, 16 * part + 16)
+                outgoing[it, i, here] = jnp.concatenate(evens, 0).astype(BF16)
+                outgoing[it, i + 1, here] = jnp.concatenate(odds, 0).astype(BF16)
+            for slot in order:
+                product_copy(it, slot, part).start()
         products[it, 0] = outgoing[it, 0]
 
-        for copy in halo_copies(it):
-            copy.wait_recv()
-        for c in range(4):
-            def write_field(l, v, c=c):
-                beside[0, c, l] = v * beside_mask
-
-            unpack_halo(it, c, write_field)
         if it == 0:
+            for copy in halo_copies(it, True) + halo_copies(it):
+                copy.wait_recv()
+            unpack_fields(it, 0, half // 2)
             for c in range(2):
                 def write_source(l, v, c=c):
                     coef[2 + c, 1, l] = v
@@ -442,11 +484,20 @@
                 coef[4, 1, l] = look(weight_table, lab)
 
             unpack_halo(0, 6, write_coef)
+        else:
+            for copy in halo_copies(it, True):
+                copy.wait_recv()
+            unpack_fields(it, 0, 2)
+        final = it == ITERS - 1
         for level in range(SWEEPS):
-            sweep_inside(level)
+            sweep_inside(level, final)
+        if not final:
+            for c in range(4):
+                pack_halo(it + 1, c, lambda l, c=c: own[0, c, l], 2)
 
         for slot in order:
-            product_copy(it, slot).wait_recv()
+            product_copy(it, slot, 0).wait_recv()
+            product_copy(it, slot, 1).wait_recv()
         owner = owner_s[0, me_s]
         owner_dx = lax.rem(lax.rem(owner, nx) - my_x + nx, nx)
         owner_dy = lax.rem(lax.div(owner, nx) - my_y + ny, ny)
@@ -463,17 +514,15 @@
         ghosts = ghost_copies(it)
         for copy in ghosts:
             copy.start()
+        if not final:
+            for copy in halo_copies(it + 1):
+                copy.start()
         trace.wait_send()
-        for copy in ghosts[3:]:
-            copy.wait_recv()
-        right_ghosts = [
-            right_own,
-            [jnp.where(upper, right_in[it, 1, c], right_in[it, 0, c]) for c in range(4)],
-        ]
-        for level in range(SWEEPS):
-            sweep_end(level, right_ghosts, False)
         for copy in ghosts[:3]:
             copy.wait_recv()
+        if final:
+            for copy in ghosts[3:]:
+                copy.wait_recv()
         left_ghosts = [
             [left_in[it, 0, c] * not_first for c in range(4)],
             [
@@ -481,24 +530,49 @@
                 for c in range(4)
             ],
         ]
-        for level in range(SWEEPS):
-            sweep_end(level, left_ghosts, True)
-        if it + 1 < ITERS:
+        if final:
+            for level in range(SWEEPS):
+                sweep_end(level, left_ghosts, True, final)
+                if level == 0:
+                    right_ghosts = [
+                        right_own,
+                        [
+                            jnp.where(upper, right_in[it, 1, c], right_in[it, 0, c])
+                            for c in range(4)
+                        ],
+                    ]
+                sweep_end(level, right_ghosts, False, final)
+        else:
+            for level in range(SWEEPS):
+                sweep_end(level, left_ghosts, True, final)
             trace_copy(it + 1).start()
+            for copy in ghosts[3:]:
+                copy.wait_recv()
+            right_ghosts = [
+                right_own,
+                [jnp.where(upper, right_in[it, 1, c], right_in[it, 0, c]) for c in range(4)],
+            ]
+            for level in range(SWEEPS):
+                sweep_end(level, right_ghosts, False, final)
+
+    for it in range(ITERS):
         for slot in order:
             jump_copy(it, slot).wait_send()
-            product_copy(it, slot).wait_send()
-        for copy in ghosts + halo_copies(it):
+            product_copy(it, slot, 0).wait_send()
+            product_copy(it, slot, 1).wait_send()
+        for copy in ghost_copies(it) + halo_copies(it) + halo_copies(it, True):
             copy.wait_send()
 
-    stores = [
-        pltpu.make_async_copy(own.at[0, 0:2], forward_h, store_sem.at[0]),
-        pltpu.make_async_copy(own.at[0, 2:4], adjoint_h, store_sem.at[1]),
+
+def store_kernel(forward_v, adjoint_v, forward_h, adjoint_h, sem):
+    copies = [
+        pltpu.make_async_copy(forward_v, forward_h, sem.at[0]),
+        pltpu.make_async_copy(adjoint_v, adjoint_h, sem.at[1]),
     ]
-    for store in stores:
-        store.start()
-    for store in stores:
-        store.wait()
+    for copy in copies:
+        copy.start()
+    for copy in copies:
+        copy.wait()
 
 
 def solution(mesh):
@@ -519,16 +593,36 @@
         layers = labels.shape[0]
         points = pairs.shape[-1]
         slots = n_sub
-        smem = pl.BlockSpec(memory_space=pltpu.SMEM)
-        hbm = pl.BlockSpec(memory_space=pl.ANY)
+        hbm = pl.BlockSpec(memory_space=pltpu.HBM)
+        vmem = pl.BlockSpec(memory_space=pltpu.VMEM)
         out = jax.ShapeDtypeStruct((2,) + labels.shape, F32)
         dma = pltpu.SemaphoreType.DMA
-        return pl.pallas_call(
+        operands = [
+            pltpu.with_memory_space_constraint(operand, pltpu.HBM)
+            for operand in (
+                pairs[0],
+                block_index,
+                wavenumber2,
+                absorption,
+                design_weight,
+                pairs.reshape(8, 128),
+                start_fields,
+                source,
+                labels,
+                blocks,
+            )
+        ]
+        results = pl.pallas_call(
             functools.partial(kernel, (n_dom, n_sub, nx)),
             out_shape=(out, out),
-            in_specs=[smem] * 5 + [hbm] * 5,
-            out_specs=(hbm, hbm),
+            in_specs=[hbm] * 10,
+            out_specs=(vmem, vmem),
             scratch_shapes=[
+                pltpu.SMEM((1, points), jnp.int32),
+                pltpu.SMEM(block_index.shape, jnp.int32),
+                pltpu.SMEM(wavenumber2.shape, F32),
+                pltpu.SMEM(absorption.shape, F32),
+                pltpu.SMEM(design_weight.shape, F32),
                 pltpu.VMEM((8, 128), jnp.int32),
                 pltpu.VMEM((2, 4, layers, 8, 128), F32),
                 pltpu.VMEM((2, 4, layers, 8, 128), F32),
@@ -548,33 +642,29 @@
                 pltpu.VMEM((ITERS, 2, 4, 8, 128), F32),
                 pltpu.VMEM((4, 7, layers // 4, 16, 128), BF16),
                 pltpu.VMEM((4, 7, layers // 4, 16, 128), BF16),
-                dma((5,)),
+                dma((10,)),
                 dma((2, ITERS)),
                 dma((ITERS, slots)),
                 dma((ITERS, slots)),
-                dma((ITERS, slots)),
-                dma((ITERS, slots)),
+                dma((ITERS, slots, 2)),
+                dma((ITERS, slots, 2)),
                 dma((ITERS, 5)),
                 dma((ITERS, 5)),
-                dma((ITERS, 2)),
-                dma((ITERS, 2)),
-                dma((2,)),
+                dma((2 * ITERS, 2)),
+                dma((2 * ITERS, 2)),
             ],
             compiler_params=pltpu.CompilerParams(
-                collective_id=0, has_side_effects=True, vmem_limit_bytes=48 * 1024 * 1024
+                collective_id=0, has_side_effects=True, vmem_limit_bytes=20 * 1024 * 1024
             ),
-        )(
-            pairs[0],
-            block_index,
-            wavenumber2,
-            absorption,
-            design_weight,
-            pairs.reshape(8, 128),
-            start_fields,
-            source,
-            labels,
-            blocks,
-        )
+        )(*operands)
+        return pl.pallas_call(
+            store_kernel,
+            out_shape=(out, out),
+            in_specs=[vmem, vmem],
+            out_specs=(hbm, hbm),
+            scratch_shapes=[dma((2,))],
+            compiler_params=pltpu.CompilerParams(vmem_limit_bytes=4 * 1024 * 1024),
+        )(*results)
 
     placed = (
         P(None, "dom", "sub", None),

time: 61.8 us -> 50.4 us (0.82)
  local copies, waits for them, and re-layouts: 9.79 us -> 0 us
  Pallas kernels: 50.5 us -> 49.5 us
    unnamed x20 -> x0, local copies, waits for them, and re-layouts: 9.79 us -> none
    pallas_call x1, Pallas kernels: 50.5 us -> 48.7 us  [per_device(): pl.pallas_call(functools.partial(kernel, (n_dom, n_sub, nx)), out_shape=(...]
    pallas_call x0 -> x1, Pallas kernels: none -> 0.81 us  [per_device(): pl.pallas_call(store_kernel, out_shape=(out, out), in_specs=[vmem, vmem],...]
where the time goes in v2:
time: 50.4 us; the launch traced here: 50.1 us
  Pallas kernels  49.5 us (98%)
  between operations  0.64 us (1%)
    pallas_call x1, Pallas kernels, per_device(): pl.pallas_call(functools.partial(kernel, (n_dom, n_sub, nx)), out_shape=(...  48.7 us

profile of v2, /device:TPU:1, one launch (start us, length us, event | category | flops | bytes accessed | tf_op | source)
XLA Modules:
  0.0 50.1 jit_solution(4908285776505604716)
XLA Ops:
  0.6 48.7 %shard_map.104 = (f32[2,32,8,128]{3,2,1,0:T(8,128)S(1)}, f32[2,32,8,128]{3,2,1,0:T(8,128)S(1)}) custom-call(s32[1,1024]{1,0:T(1,128)} %bitcast.2, s32[1,16]{1,0:T(1,128)} %owner_h.1, f32[16]{0:T(128)} %wave_h.1, f32[16]{0:T(128)} %absorb_h.1, f32[16]{0:T(128)} %design_h.1, s32[8,128]{1,0:T(8,128)} %bitcast.3, f32[4,32,8,128]{3,2,1,0:T(8,128)} %fields_h.1, ...), custom_call_target="tpu_custom_call" | custom-call | tf_op jit(solution)/shard_map/pallas_call | solution.py:615
  49.3 0.8 %shard_map.105 = (f32[2,32,8,128]{3,2,1,0:T(8,128)}, f32[2,32,8,128]{3,2,1,0:T(8,128)}) custom-call(f32[2,32,8,128]{3,2,1,0:T(8,128)S(1)} %get-tuple-element.4.forward_v, f32[2,32,8,128]{3,2,1,0:T(8,128)S(1)} %get-tuple-element.5.adjoint_v), custom_call_target="tpu_custom_call" | custom-call | tf_op jit(solution)/shard_map/pallas_call | solution.py:660

commit v3 on v2

--- a/solution.py
+++ b/solution.py
@@ -54,9 +54,11 @@
     rows32,
     face,
     left_out,
-    right_out,
     left_in,
-    right_in,
+    side_out,
+    side_in,
+    inv_out,
+    inv_in,
     halo_out,
     halo_in,
     load_sem,
@@ -67,8 +69,17 @@
     prod_recv,
     ghost_send,
     ghost_recv,
+    side_send,
+    side_recv,
+    inv_send,
+    inv_recv,
     halo_send,
     halo_recv,
+    nxt,
+    nxt_coef,
+    nxt_out,
+    nxt_send,
+    nxt_recv,
 ):
     n_dom, n_sub, nx = shape
     ny = n_sub // nx
@@ -83,6 +94,12 @@
     def member(slot):
         dx, dy = offsets[slot]
         return lax.rem(my_y + dy, ny) * nx + lax.rem(my_x + dx, nx)
+
+    barrier = pltpu.get_barrier_semaphore()
+    greeted = [(me_d, member(slot)) for slot in order]
+    greeted += [(before_d, me_s), (after_d, me_s)]
+    for device in greeted:
+        pl.semaphore_signal(barrier, inc=1, device_id=device, device_id_type=MESH)
 
     small_loads = [
         pltpu.make_async_copy(src, dst, load_sem.at[5 + k])
@@ -108,14 +125,6 @@
     for load in loads[:4]:
         load.start()
 
-    barrier = pltpu.get_barrier_semaphore()
-    greeted = [(me_d, member(slot)) for slot in order]
-    for dom in (before_d, after_d):
-        for sub in (before_s, me_s, after_s):
-            greeted.append((dom, sub))
-    for device in greeted:
-        pl.semaphore_signal(barrier, inc=1, device_id=device, device_id_type=MESH)
-
     row = lax.broadcasted_iota(jnp.int32, (8, 128), 0)
     lane = lax.broadcasted_iota(jnp.int32, (8, 128), 1)
     upper = row < 4
@@ -129,15 +138,48 @@
     def roll4(value):
         return pltpu.roll(value, 4, 0)
 
-    def trace_copy(it):
+    depth = nxt.shape[3]
+
+    def trace_copy():
         return pltpu.make_async_remote_copy(
-            src_ref=fields_h.at[:, 0] if it == 0 else own.at[0, :, 0],
-            dst_ref=facing_in.at[it],
-            send_sem=trace_sem.at[0, it],
-            recv_sem=trace_sem.at[1, it],
+            src_ref=fields_h.at[:, 0],
+            dst_ref=facing_in,
+            send_sem=trace_sem.at[0],
+            recv_sem=trace_sem.at[1],
             device_id=(before_d, me_s),
             device_id_type=MESH,
         )
+
+    def next_copies():
+        copies = []
+        for k, (src, dst) in enumerate(
+            (
+                (fields_h.at[:, 0:depth], nxt.at[0, 0]),
+                (coef.at[:, 0, 0 : depth - 1], nxt_coef.at[:, 0]),
+                (nxt_out, nxt.at[0, 1]),
+                (coef.at[:, 1, 0 : depth - 1], nxt_coef.at[:, 1]),
+            )
+        ):
+            copies.append(
+                pltpu.make_async_remote_copy(
+                    src_ref=src,
+                    dst_ref=dst,
+                    send_sem=nxt_send.at[k],
+                    recv_sem=nxt_recv.at[k],
+                    device_id=(before_d, me_s),
+                    device_id_type=MESH,
+                )
+            )
+        return copies
+
+    def source_of(slot):
+        dx, dy = offsets[slot]
+        return lax.rem(my_y + ny - dy, ny) * nx + lax.rem(my_x + nx - dx, nx)
+
+    def slot_of(member_index):
+        dx = lax.rem(lax.rem(member_index, nx) - my_x + nx, nx)
+        dy = lax.rem(lax.div(member_index, nx) - my_y + ny, ny)
+        return dy * nx + dx
 
     def jump_copy(it, slot):
         return pltpu.make_async_remote_copy(
@@ -150,40 +192,45 @@
         )
 
     def product_copy(it, slot, part):
-        dx, dy = offsets[slot]
-        back = lax.rem(my_y + ny - dy, ny) * nx + lax.rem(my_x + nx - dx, nx)
+        back = source_of(slot)
         rows = pl.ds(16 * part, 16)
         return pltpu.make_async_remote_copy(
-            src_ref=outgoing.at[it, slot, rows],
-            dst_ref=products.at[it, slot, rows],
+            src_ref=outgoing.at[it, pl.ds(back, 3), rows],
+            dst_ref=products.at[it, slot, :, rows],
             send_sem=prod_send.at[it, slot, part],
             recv_sem=prod_recv.at[it, slot, part],
             device_id=(me_d, back),
             device_id_type=MESH,
         )
 
-    def ghost_copies(it):
-        copies = []
-        for k, (src, dst, device) in enumerate(
-            (
-                (left_out, left_in.at[it, 0], (after_d, me_s)),
-                (left_out, left_in.at[it, 1], (after_d, after_s)),
-                (left_out, left_in.at[it, 2], (after_d, before_s)),
-                (right_out, right_in.at[it, 0], (me_d, after_s)),
-                (right_out, right_in.at[it, 1], (me_d, before_s)),
-            )
-        ):
-            copies.append(
-                pltpu.make_async_remote_copy(
-                    src_ref=src.at[it],
-                    dst_ref=dst,
-                    send_sem=ghost_send.at[it, k],
-                    recv_sem=ghost_recv.at[it, k],
-                    device_id=device,
-                    device_id_type=MESH,
-                )
-            )
-        return copies
+    def ghost_copy(it):
+        return pltpu.make_async_remote_copy(
+            src_ref=left_out.at[it],
+            dst_ref=left_in.at[it],
+            send_sem=ghost_send.at[it],
+            recv_sem=ghost_recv.at[it],
+            device_id=(after_d, me_s),
+            device_id_type=MESH,
+        )
+
+    def beside_copies(src, dst, send_sem, recv_sem):
+        return [
+            pltpu.make_async_remote_copy(
+                src_ref=src,
+                dst_ref=dst.at[k],
+                send_sem=send_sem.at[k],
+                recv_sem=recv_sem.at[k],
+                device_id=(me_d, sub),
+                device_id_type=MESH,
+            )
+            for k, sub in enumerate((after_s, before_s))
+        ]
+
+    def side_copies(it):
+        return beside_copies(side_out.at[it], side_in.at[it], side_send.at[it], side_recv.at[it])
+
+    def inverse_copies():
+        return beside_copies(inv_out, inv_in, inv_send, inv_recv)
 
     def halo_copies(it, second=False):
         groups = halo_out.shape[2]
@@ -250,7 +297,7 @@
         high = jnp.where(lane == 127, 0.0, pltpu.roll(v, 127, 1))
         return low + high
 
-    def relax(cur, across, layer, tiles):
+    def relax(cur, across, layer, tiles, table):
         sums = [[None] * 4 for _ in range(2)]
         for c in range(4):
             a, b = cur[0][c], cur[1][c]
@@ -266,10 +313,10 @@
                 sums[t][c] = across[t][c] + y_sum + z_sum(v)
         results = []
         for t in tiles:
-            rr, ri = coef[0, t, layer], coef[1, t, layer]
-            w = coef[4, t, layer]
-            fr = coef[2, t, layer] + sums[t][0]
-            fi = coef[3, t, layer] + sums[t][1]
+            rr, ri = table[0, t, layer], table[1, t, layer]
+            w = table[4, t, layer]
+            fr = table[2, t, layer] + sums[t][0]
+            fi = table[3, t, layer] + sums[t][1]
             ar = w * cur[t][0] + sums[t][2]
             ai = w * cur[t][1] + sums[t][3]
             results.append(
@@ -295,7 +342,7 @@
         for i in range(count):
             low, cur, high = values[i], values[i + 1], values[i + 2]
             across = [[low[t][c] + high[t][c] for c in range(4)] for t in range(2)]
-            results = relax(cur, across, first + i, tiles)
+            results = relax(cur, across, first + i, tiles, coef)
             for t, result in zip(tiles, results):
                 for c in range(4):
                     put(level, final, t, c, first + i, result[c])
@@ -328,10 +375,27 @@
         for layer in span:
             low, cur, high = values[layer - 1], values[layer], values[layer + 1]
             across = [[low[t][c] + high[t][c] for c in range(4)] for t in range(2)]
-            results = relax(cur, across, layer, tiles)
+            results = relax(cur, across, layer, tiles, coef)
             for t, result in zip(tiles, results):
                 for c in range(4):
                     put(level, final, t, c, layer, result[c])
+
+    def next_sweep(level, span, ghosts):
+        tiles = (0, 1) if level < SWEEPS - 1 else (0,)
+        src, dst = level % 2, (level + 1) % 2
+
+        def fetch(layer):
+            if layer < 0:
+                return ghosts
+            return [[nxt[src, t, c, layer] for c in range(4)] for t in range(2)]
+
+        values = {layer: fetch(layer) for layer in range(span[0] - 1, span[-1] + 2)}
+        for layer in span:
+            low, cur, high = values[layer - 1], values[layer], values[layer + 1]
+            across = [[low[t][c] + high[t][c] for c in range(4)] for t in range(2)]
+            for t, result in zip(tiles, relax(cur, across, layer, tiles, nxt_coef)):
+                for c in range(4):
+                    nxt[dst, t, c, layer] = result[c]
 
     def coefficients_of(tile, mask=None, read=None):
         def step(layer, carry):
@@ -347,7 +411,8 @@
         lax.fori_loop(0, layers, step, 0, unroll=4)
 
     pl.semaphore_wait(barrier, len(greeted))
-    trace_copy(0).start()
+    trace_copy().start()
+    next_copies()[0].start()
     for load in loads[1:4]:
         load.wait()
     loads[4].start()
@@ -396,27 +461,51 @@
             out = jnp.where(index_row == r, look(source_row, index_lane), out)
         return out
 
+    def left_ghosts(it):
+        return [[left_in[it, t, c] * not_first for c in range(4)] for t in range(2)]
+
     for it in range(ITERS):
-        trace = trace_copy(it)
-        trace.wait_recv()
+        outgoing[it, 0] = jnp.zeros((32, 128), BF16)
+        outgoing[it, n_sub + 1] = jnp.zeros((32, 128), BF16)
+
+    for it in range(ITERS):
+        if it == 0:
+            trace_copy().wait_recv()
         facing = []
         for c in range(4):
-            taken = gather_points(lambda r: facing_in[it, c, r : r + 1, :], pairs)
+            taken = gather_points(
+                lambda r: (facing_in[c] if it == 0 else nxt[0, 0, c, 0])[r : r + 1, :], pairs
+            )
             taken = taken * not_last
             facing.append(taken)
-            face[c] = taken
-            rows32[pl.ds(c, 8, stride=4), :] = taken - own[0, c, layers - 1]
-        jumps[it, 0] = rows32[...].astype(BF16)
+            face[1, c] = taken
+            rows32[0, pl.ds(c, 8, stride=4), :] = taken - own[0, c, layers - 1]
+        jumps[it, 0] = rows32[0].astype(BF16)
         for slot in order:
             jump_copy(it, slot).start()
+        for t in range(2):
+            last = [own[0, 2 * t + k, layers - 1] for k in range(2)]
+            side_out[it, 16 * t : 16 * t + 16] = jnp.concatenate(last, 0).astype(BF16)
+            side_out[it, 32 + 16 * t : 48 + 16 * t] = jnp.concatenate(
+                facing[2 * t : 2 * t + 2], 0
+            ).astype(BF16)
+        for copy in side_copies(it):
+            copy.start()
 
         if it == 0:
             for copy in halo_copies(0):
                 copy.start()
             coefficients_of(0, read=lambda l: labels[l])
+            next_copies()[1].start()
             inverse = lax.fori_loop(0, 64, place, jnp.zeros((8, 128), jnp.int32))
+            inv_out[...] = inverse
+            for copy in inverse_copies():
+                copy.start()
             loads[4].wait()
         else:
+            ghost_copy(0).wait_recv()
+            for level in range(SWEEPS):
+                sweep_end(level, left_ghosts(0), True, False)
             for c in range(4):
                 pack_halo(it, c, lambda l, c=c: own[0, c, l], 0, 2)
             for copy in halo_copies(it, True):
@@ -424,6 +513,16 @@
             for copy in halo_copies(it):
                 copy.wait_recv()
             unpack_fields(it, 2, half // 2)
+        contract = (((1,), (1,)), ((), ()))
+        width = block.shape[1] // 2
+
+        def product(columns):
+            return lax.dot_general(
+                stacked[0], block[0, columns], contract, preferred_element_type=F32
+            ) + lax.dot_general(
+                stacked[1], block[1, columns], contract, preferred_element_type=F32
+            )
+
         for slot in order:
             jump_copy(it, slot).wait_recv()
         for i in range(0, n_sub, 4):
@@ -437,21 +536,13 @@
                     v = jnp.where(upper, roll4(a) if odd else a, b if odd else roll4(b))
                     plain.append(v)
                     turned.append(jnp.where(even, -pltpu.roll(v, 7, 0), pltpu.roll(v, 1, 0)))
-                stacked[0, 4 * i : 4 * i + 16, r * 128 : r * 128 + 128] = jnp.concatenate(
-                    plain, 0
-                ).astype(BF16)
-                stacked[1, 4 * i : 4 * i + 16, r * 128 : r * 128 + 128] = jnp.concatenate(
-                    turned, 0
-                ).astype(BF16)
-        contract = (((1,), (1,)), ((), ()))
-        width = 512
+                columns = pl.ds(r * 128, 128)
+                rows = pl.ds(4 * i, 16)
+                stacked[0, rows, columns] = jnp.concatenate(plain, 0).astype(BF16)
+                stacked[1, rows, columns] = jnp.concatenate(turned, 0).astype(BF16)
         for part in range(2):
-            span = pl.ds(width * part, width)
-            total = lax.dot_general(
-                stacked[0], block[0, span, :], contract, preferred_element_type=F32
-            ) + lax.dot_general(
-                stacked[1], block[1, span, :], contract, preferred_element_type=F32
-            )
+            total = product(pl.ds(width * part, width))
+            here = slice(16 * part, 16 * part + 16)
             for i in range(0, n_sub, 2):
                 rows = total[4 * i : 4 * i + 8]
                 evens, odds = [], []
@@ -460,12 +551,12 @@
                     b = rows[:, 256 * k + 128 : 256 * k + 256]
                     evens.append(jnp.where(upper, a, roll4(b)))
                     odds.append(jnp.where(upper, roll4(a), b))
-                here = slice(16 * part, 16 * part + 16)
-                outgoing[it, i, here] = jnp.concatenate(evens, 0).astype(BF16)
-                outgoing[it, i + 1, here] = jnp.concatenate(odds, 0).astype(BF16)
+                outgoing[it, source_of(i) + 1, here] = jnp.concatenate(evens, 0).astype(BF16)
+                outgoing[it, source_of(i + 1) + 1, here] = jnp.concatenate(odds, 0).astype(BF16)
             for slot in order:
                 product_copy(it, slot, part).start()
-        products[it, 0] = outgoing[it, 0]
+        for k in range(3):
+            products[it, 0, k] = outgoing[it, me_s + k]
 
         if it == 0:
             for copy in halo_copies(it, True) + halo_copies(it):
@@ -484,6 +575,11 @@
                 coef[4, 1, l] = look(weight_table, lab)
 
             unpack_halo(0, 6, write_coef)
+            for c in range(4):
+                for layer in range(depth):
+                    nxt_out[c, layer] = beside[0, c, layer]
+            for copy in next_copies()[2:]:
+                copy.start()
         else:
             for copy in halo_copies(it, True):
                 copy.wait_recv()
@@ -494,74 +590,80 @@
         if not final:
             for c in range(4):
                 pack_halo(it + 1, c, lambda l, c=c: own[0, c, l], 2)
-
+            for copy in halo_copies(it + 1):
+                copy.start()
+
+        if not final:
+            for copy in next_copies():
+                copy.wait_recv()
+            next_sweep(0, range(1, depth - 1), None)
+            next_sweep(1, range(2, depth - 2), None)
+            for copy in inverse_copies():
+                copy.wait_recv()
+            inverse_beside = jnp.where(upper, inv_in[1], inv_in[0])
+        for copy in side_copies(it):
+            copy.wait_recv()
         for slot in order:
             product_copy(it, slot, 0).wait_recv()
             product_copy(it, slot, 1).wait_recv()
-        owner = owner_s[0, me_s]
-        owner_dx = lax.rem(lax.rem(owner, nx) - my_x + nx, nx)
-        owner_dy = lax.rem(lax.div(owner, nx) - my_y + ny, ny)
-        rows32[...] = products[it, owner_dy * nx + owner_dx].astype(F32)
-        right_own, back = [], []
+        for k in range(3):
+            owner = owner_s[0, lax.rem(me_s + n_sub + k - 1, n_sub)]
+            rows32[k] = products[it, slot_of(owner), k].astype(F32)
+        right = [[], []]
         for c in range(4):
-            moved = rows32[pl.ds(c, 8, stride=4), :]
-            right = (face[c] + moved) * not_last
-            right_own.append(right)
-            right_out[it, c] = right
-            face[c] = own[0, c, layers - 1] - moved
+            moved = [rows32[k, pl.ds(c, 8, stride=4), :] for k in range(3)]
+            pair = pl.ds(16 * (c // 2), 16)
+            half_rows = slice(8 * (c % 2), 8 * (c % 2) + 8)
+            lasts = [side_in[it, k, pair].astype(F32)[half_rows] for k in range(2)]
+            pair = pl.ds(32 + 16 * (c // 2), 16)
+            faces = [side_in[it, k, pair].astype(F32)[half_rows] for k in range(2)]
+            right[0].append((face[1, c] + moved[1]) * not_last)
+            right[1].append(
+                jnp.where(upper, faces[1] + moved[2], faces[0] + moved[0]) * not_last
+            )
+            face[1, c] = own[0, c, layers - 1] - moved[1]
+            face[0, c] = lasts[0] - moved[0]
+            face[2, c] = lasts[1] - moved[2]
+        left = [[], []]
         for c in range(4):
-            left_out[it, c] = gather_points(lambda r: face[c, r : r + 1, :], inverse)
-        ghosts = ghost_copies(it)
-        for copy in ghosts:
-            copy.start()
+            left[0].append(gather_points(lambda r: face[1, c, r : r + 1, :], inverse))
+            left[1].append(
+                gather_points(
+                    lambda r: jnp.where(
+                        upper,
+                        jnp.broadcast_to(face[2, c, r : r + 1, :], (8, 128)),
+                        jnp.broadcast_to(face[0, c, r : r + 1, :], (8, 128)),
+                    ),
+                    inverse_beside,
+                )
+            )
+            left_out[it, 0, c] = left[0][c]
+            left_out[it, 1, c] = left[1][c]
+        ghost_copy(it).start()
         if not final:
-            for copy in halo_copies(it + 1):
-                copy.start()
-        trace.wait_send()
-        for copy in ghosts[:3]:
-            copy.wait_recv()
-        if final:
-            for copy in ghosts[3:]:
-                copy.wait_recv()
-        left_ghosts = [
-            [left_in[it, 0, c] * not_first for c in range(4)],
-            [
-                jnp.where(upper, left_in[it, 2, c], left_in[it, 1, c]) * not_first
-                for c in range(4)
-            ],
-        ]
-        if final:
             for level in range(SWEEPS):
-                sweep_end(level, left_ghosts, True, final)
-                if level == 0:
-                    right_ghosts = [
-                        right_own,
-                        [
-                            jnp.where(upper, right_in[it, 1, c], right_in[it, 0, c])
-                            for c in range(4)
-                        ],
-                    ]
-                sweep_end(level, right_ghosts, False, final)
+                next_sweep(level, ((0,), (0, 1), (0, 1), (0,))[level], left)
+                sweep_end(level, right, False, final)
         else:
+            trace_copy().wait_send()
+            for copy in next_copies():
+                copy.wait_send()
+            for k in range(ITERS):
+                for slot in order:
+                    jump_copy(k, slot).wait_send()
+                    product_copy(k, slot, 0).wait_send()
+                    product_copy(k, slot, 1).wait_send()
+                for copy in side_copies(k) + halo_copies(k) + halo_copies(k, True):
+                    copy.wait_send()
+            for copy in inverse_copies():
+                copy.wait_send()
+            ghost_copy(0).wait_send()
+            ghost_copy(it).wait_recv()
+            left = left_ghosts(it)
             for level in range(SWEEPS):
-                sweep_end(level, left_ghosts, True, final)
-            trace_copy(it + 1).start()
-            for copy in ghosts[3:]:
-                copy.wait_recv()
-            right_ghosts = [
-                right_own,
-                [jnp.where(upper, right_in[it, 1, c], right_in[it, 0, c]) for c in range(4)],
-            ]
-            for level in range(SWEEPS):
-                sweep_end(level, right_ghosts, False, final)
-
-    for it in range(ITERS):
-        for slot in order:
-            jump_copy(it, slot).wait_send()
-            product_copy(it, slot, 0).wait_send()
-            product_copy(it, slot, 1).wait_send()
-        for copy in ghost_copies(it) + halo_copies(it) + halo_copies(it, True):
-            copy.wait_send()
+                sweep_end(level, left, True, final)
+                sweep_end(level, right, False, final)
+            ghost_copy(it).wait_send()
 
 
 def store_kernel(forward_v, adjoint_v, forward_h, adjoint_h, sem):
@@ -629,29 +731,40 @@
                 pltpu.VMEM((5, 2, layers, 8, 128), F32),
                 pltpu.VMEM((layers, 8, 128), jnp.int32),
                 pltpu.VMEM((2, points, points), BF16),
-                pltpu.VMEM((ITERS, 4, 8, 128), F32),
+                pltpu.VMEM((4, 8, 128), F32),
                 pltpu.VMEM((ITERS, slots, 32, 128), BF16),
                 pltpu.VMEM((2, 4 * slots, points), BF16),
-                pltpu.VMEM((ITERS, slots, 32, 128), BF16),
-                pltpu.VMEM((ITERS, slots, 32, 128), BF16),
-                pltpu.VMEM((32, 128), F32),
-                pltpu.VMEM((4, 8, 128), F32),
-                pltpu.VMEM((ITERS, 4, 8, 128), F32),
-                pltpu.VMEM((ITERS, 4, 8, 128), F32),
-                pltpu.VMEM((ITERS, 3, 4, 8, 128), F32),
+                pltpu.VMEM((ITERS, slots + 2, 32, 128), BF16),
+                pltpu.VMEM((ITERS, slots, 3, 32, 128), BF16),
+                pltpu.VMEM((3, 32, 128), F32),
+                pltpu.VMEM((3, 4, 8, 128), F32),
                 pltpu.VMEM((ITERS, 2, 4, 8, 128), F32),
+                pltpu.VMEM((ITERS, 2, 4, 8, 128), F32),
+                pltpu.VMEM((ITERS, 64, 128), BF16),
+                pltpu.VMEM((ITERS, 2, 64, 128), BF16),
+                pltpu.VMEM((8, 128), jnp.int32),
+                pltpu.VMEM((2, 8, 128), jnp.int32),
                 pltpu.VMEM((4, 7, layers // 4, 16, 128), BF16),
                 pltpu.VMEM((4, 7, layers // 4, 16, 128), BF16),
                 dma((10,)),
-                dma((2, ITERS)),
+                dma((2,)),
                 dma((ITERS, slots)),
                 dma((ITERS, slots)),
                 dma((ITERS, slots, 2)),
                 dma((ITERS, slots, 2)),
-                dma((ITERS, 5)),
-                dma((ITERS, 5)),
+                dma((ITERS,)),
+                dma((ITERS,)),
+                dma((ITERS, 2)),
+                dma((ITERS, 2)),
+                dma((2,)),
+                dma((2,)),
                 dma((2 * ITERS, 2)),
                 dma((2 * ITERS, 2)),
+                pltpu.VMEM((2, 2, 4, SWEEPS + 1, 8, 128), F32),
+                pltpu.VMEM((5, 2, SWEEPS, 8, 128), F32),
+                pltpu.VMEM((4, SWEEPS + 1, 8, 128), F32),
+                dma((4,)),
+                dma((4,)),
             ],
             compiler_params=pltpu.CompilerParams(
                 collective_id=0, has_side_effects=True, vmem_limit_bytes=20 * 1024 * 1024

time: 50.4 us -> 42.6 us (0.85)
  Pallas kernels: 49.5 us -> 41.9 us
    pallas_call x1, Pallas kernels: 48.7 us -> 41.1 us  [per_device(): pl.pallas_call(functools.partial(kernel, (n_dom, n_sub, nx)), out_shape=(...]
where the time goes in v3:
time: 42.6 us
  Pallas kernels  41.9 us (98%)
  between operations  0.64 us (2%)
    pallas_call x1, Pallas kernels, per_device(): pl.pallas_call(functools.partial(kernel, (n_dom, n_sub, nx)), out_shape=(...  41.1 us

profile of v3, /device:TPU:1, one launch (start us, length us, event | category | flops | bytes accessed | tf_op | source)
XLA Modules:
  0.0 42.6 jit_solution(7371303024547800566)
XLA Ops:
  0.6 41.1 %shard_map.104 = (f32[2,32,8,128]{3,2,1,0:T(8,128)S(1)}, f32[2,32,8,128]{3,2,1,0:T(8,128)S(1)}) custom-call(s32[1,1024]{1,0:T(1,128)} %bitcast.2, s32[1,16]{1,0:T(1,128)} %owner_h.1, f32[16]{0:T(128)} %wave_h.1, f32[16]{0:T(128)} %absorb_h.1, f32[16]{0:T(128)} %design_h.1, s32[8,128]{1,0:T(8,128)} %bitcast.3, f32[4,32,8,128]{3,2,1,0:T(8,128)} %fields_h.1, ...), custom_call_target="tpu_custom_call" | custom-call | tf_op jit(solution)/shard_map/pallas_call | solution.py:717
  41.8 0.8 %shard_map.105 = (f32[2,32,8,128]{3,2,1,0:T(8,128)}, f32[2,32,8,128]{3,2,1,0:T(8,128)}) custom-call(f32[2,32,8,128]{3,2,1,0:T(8,128)S(1)} %get-tuple-element.4.forward_v, f32[2,32,8,128]{3,2,1,0:T(8,128)S(1)} %get-tuple-element.5.adjoint_v), custom_call_target="tpu_custom_call" | custom-call | tf_op jit(solution)/shard_map/pallas_call | solution.py:773

commit v4 on v3

--- a/solution.py
+++ b/solution.py
@@ -46,6 +46,7 @@
     coef,
     labels,
     block,
+    turned_block,
     facing_in,
     jumps,
     stacked,
@@ -96,8 +97,8 @@
         return lax.rem(my_y + dy, ny) * nx + lax.rem(my_x + dx, nx)
 
     barrier = pltpu.get_barrier_semaphore()
-    greeted = [(me_d, member(slot)) for slot in order]
-    greeted += [(before_d, me_s), (after_d, me_s)]
+    greeted = [(me_d, member(slot)) for slot in reversed(order)]
+    greeted = [(before_d, me_s), (after_d, me_s)] + greeted
     for device in greeted:
         pl.semaphore_signal(barrier, inc=1, device_id=device, device_id_type=MESH)
 
@@ -185,23 +186,46 @@
         return pltpu.make_async_remote_copy(
             src_ref=jumps.at[it, 0],
             dst_ref=jumps.at[it, slot],
-            send_sem=jump_send.at[it, slot],
-            recv_sem=jump_recv.at[it, slot],
+            send_sem=jump_send.at[it],
+            recv_sem=jump_recv.at[it],
             device_id=(me_d, member(slot)),
             device_id_type=MESH,
         )
 
-    def product_copy(it, slot, part):
+    def product_copy(it, slot):
         back = source_of(slot)
-        rows = pl.ds(16 * part, 16)
         return pltpu.make_async_remote_copy(
-            src_ref=outgoing.at[it, pl.ds(back, 3), rows],
-            dst_ref=products.at[it, slot, :, rows],
-            send_sem=prod_send.at[it, slot, part],
-            recv_sem=prod_recv.at[it, slot, part],
+            src_ref=outgoing.at[it, pl.ds(back, 3)],
+            dst_ref=products.at[it, slot],
+            send_sem=prod_send.at[it],
+            recv_sem=prod_recv.at[it],
             device_id=(me_d, back),
             device_id_type=MESH,
         )
+
+    def all_of(ref, send_sem, recv_sem):
+        return pltpu.make_async_remote_copy(
+            src_ref=ref,
+            dst_ref=ref,
+            send_sem=send_sem,
+            recv_sem=recv_sem,
+            device_id=(me_d, after_s),
+            device_id_type=MESH,
+        )
+
+    others = pl.ds(1, n_sub - 1)
+
+    def all_jumps(it):
+        return all_of(jumps.at[it, others], jump_send.at[it], jump_recv.at[it])
+
+    def all_products(it):
+        return all_of(products.at[it, others], prod_send.at[it], prod_recv.at[it])
+
+    def all_sides(it):
+        return all_of(side_in.at[it], side_send.at[it], side_recv.at[it])
+
+    def all_inverses():
+        return all_of(inv_in, inv_send, inv_recv)
 
     def ghost_copy(it):
         return pltpu.make_async_remote_copy(
@@ -218,8 +242,8 @@
             pltpu.make_async_remote_copy(
                 src_ref=src,
                 dst_ref=dst.at[k],
-                send_sem=send_sem.at[k],
-                recv_sem=recv_sem.at[k],
+                send_sem=send_sem,
+                recv_sem=recv_sem,
                 device_id=(me_d, sub),
                 device_id_type=MESH,
             )
@@ -232,26 +256,31 @@
     def inverse_copies():
         return beside_copies(inv_out, inv_in, inv_send, inv_recv)
 
-    def halo_copies(it, second=False):
+    def halo_part(it, second):
         groups = halo_out.shape[2]
         if it == 0:
-            items, span = ((4, 3) if second else (0, 4)), (0, groups)
-        else:
-            items, span = (0, 4), ((0, 2) if second else (2, groups - 2))
+            return (pl.ds(4, 3) if second else pl.ds(0, 4)), pl.ds(0, groups)
+        return pl.ds(0, 4), (pl.ds(0, 2) if second else pl.ds(2, groups - 2))
+
+    def halo_copies(it, second=False):
         copies = []
         for k, sub in enumerate((after_s, before_s)):
-            part = (2 * it + k, pl.ds(*items), pl.ds(*span))
+            part = (2 * it + k,) + halo_part(it, second)
             copies.append(
                 pltpu.make_async_remote_copy(
                     src_ref=halo_out.at[part],
                     dst_ref=halo_in.at[part],
-                    send_sem=halo_send.at[2 * it + second, k],
-                    recv_sem=halo_recv.at[2 * it + second, k],
+                    send_sem=halo_send.at[2 * it + second],
+                    recv_sem=halo_recv.at[2 * it + second],
                     device_id=(me_d, sub),
                     device_id_type=MESH,
                 )
             )
         return copies
+
+    def all_halos(it, second=False):
+        part = (pl.ds(2 * it, 2),) + halo_part(it, second)
+        return all_of(halo_in.at[part], halo_send.at[2 * it + second], halo_recv.at[2 * it + second])
 
     half = layers // 2
 
@@ -502,6 +531,14 @@
             for copy in inverse_copies():
                 copy.start()
             loads[4].wait()
+
+            def turn(k, carry):
+                rows = pl.ds(pl.multiple_of(128 * k, 128), 128)
+                for h in range(2):
+                    turned_block[h, :, rows] = jnp.transpose(block[h, rows, :])
+                return carry
+
+            lax.fori_loop(0, block.shape[1] // 128, turn, 0)
         else:
             ghost_copy(0).wait_recv()
             for level in range(SWEEPS):
@@ -510,21 +547,19 @@
                 pack_halo(it, c, lambda l, c=c: own[0, c, l], 0, 2)
             for copy in halo_copies(it, True):
                 copy.start()
-            for copy in halo_copies(it):
-                copy.wait_recv()
+            all_halos(it).wait_recv()
             unpack_fields(it, 2, half // 2)
-        contract = (((1,), (1,)), ((), ()))
+        contract = (((1,), (0,)), ((), ()))
         width = block.shape[1] // 2
 
         def product(columns):
             return lax.dot_general(
-                stacked[0], block[0, columns], contract, preferred_element_type=F32
+                stacked[0], turned_block[0, :, columns], contract, preferred_element_type=F32
             ) + lax.dot_general(
-                stacked[1], block[1, columns], contract, preferred_element_type=F32
-            )
-
-        for slot in order:
-            jump_copy(it, slot).wait_recv()
+                stacked[1], turned_block[1, :, columns], contract, preferred_element_type=F32
+            )
+
+        all_jumps(it).wait_recv()
         for i in range(0, n_sub, 4):
             first = [jumps[it, i + t].astype(F32) for t in range(4)]
             for r in range(8):
@@ -553,14 +588,14 @@
                     odds.append(jnp.where(upper, roll4(a), b))
                 outgoing[it, source_of(i) + 1, here] = jnp.concatenate(evens, 0).astype(BF16)
                 outgoing[it, source_of(i + 1) + 1, here] = jnp.concatenate(odds, 0).astype(BF16)
-            for slot in order:
-                product_copy(it, slot, part).start()
+        for slot in order:
+            product_copy(it, slot).start()
         for k in range(3):
             products[it, 0, k] = outgoing[it, me_s + k]
 
         if it == 0:
-            for copy in halo_copies(it, True) + halo_copies(it):
-                copy.wait_recv()
+            all_halos(it, True).wait_recv()
+            all_halos(it).wait_recv()
             unpack_fields(it, 0, half // 2)
             for c in range(2):
                 def write_source(l, v, c=c):
@@ -581,8 +616,7 @@
             for copy in next_copies()[2:]:
                 copy.start()
         else:
-            for copy in halo_copies(it, True):
-                copy.wait_recv()
+            all_halos(it, True).wait_recv()
             unpack_fields(it, 0, 2)
         final = it == ITERS - 1
         for level in range(SWEEPS):
@@ -598,14 +632,10 @@
                 copy.wait_recv()
             next_sweep(0, range(1, depth - 1), None)
             next_sweep(1, range(2, depth - 2), None)
-            for copy in inverse_copies():
-                copy.wait_recv()
+            all_inverses().wait_recv()
             inverse_beside = jnp.where(upper, inv_in[1], inv_in[0])
-        for copy in side_copies(it):
-            copy.wait_recv()
-        for slot in order:
-            product_copy(it, slot, 0).wait_recv()
-            product_copy(it, slot, 1).wait_recv()
+        all_sides(it).wait_recv()
+        all_products(it).wait_recv()
         for k in range(3):
             owner = owner_s[0, lax.rem(me_s + n_sub + k - 1, n_sub)]
             rows32[k] = products[it, slot_of(owner), k].astype(F32)
@@ -649,14 +679,15 @@
             for copy in next_copies():
                 copy.wait_send()
             for k in range(ITERS):
-                for slot in order:
-                    jump_copy(k, slot).wait_send()
-                    product_copy(k, slot, 0).wait_send()
-                    product_copy(k, slot, 1).wait_send()
-                for copy in side_copies(k) + halo_copies(k) + halo_copies(k, True):
+                for copy in (
+                    all_jumps(k),
+                    all_products(k),
+                    all_sides(k),
+                    all_halos(k),
+                    all_halos(k, True),
+                ):
                     copy.wait_send()
-            for copy in inverse_copies():
-                copy.wait_send()
+            all_inverses().wait_send()
             ghost_copy(0).wait_send()
             ghost_copy(it).wait_recv()
             left = left_ghosts(it)
@@ -731,6 +762,7 @@
                 pltpu.VMEM((5, 2, layers, 8, 128), F32),
                 pltpu.VMEM((layers, 8, 128), jnp.int32),
                 pltpu.VMEM((2, points, points), BF16),
+                pltpu.VMEM((2, points, points), BF16),
                 pltpu.VMEM((4, 8, 128), F32),
                 pltpu.VMEM((ITERS, slots, 32, 128), BF16),
                 pltpu.VMEM((2, 4 * slots, points), BF16),
@@ -748,18 +780,18 @@
                 pltpu.VMEM((4, 7, layers // 4, 16, 128), BF16),
                 dma((10,)),
                 dma((2,)),
-                dma((ITERS, slots)),
-                dma((ITERS, slots)),
-                dma((ITERS, slots, 2)),
-                dma((ITERS, slots, 2)),
                 dma((ITERS,)),
                 dma((ITERS,)),
-                dma((ITERS, 2)),
-                dma((ITERS, 2)),
-                dma((2,)),
-                dma((2,)),
-                dma((2 * ITERS, 2)),
-                dma((2 * ITERS, 2)),
+                dma((ITERS,)),
+                dma((ITERS,)),
+                dma((ITERS,)),
+                dma((ITERS,)),
+                dma((ITERS,)),
+                dma((ITERS,)),
+                dma(()),
+                dma(()),
+                dma((2 * ITERS,)),
+                dma((2 * ITERS,)),
                 pltpu.VMEM((2, 2, 4, SWEEPS + 1, 8, 128), F32),
                 pltpu.VMEM((5, 2, SWEEPS, 8, 128), F32),
                 pltpu.VMEM((4, SWEEPS + 1, 8, 128), F32),

time: 42.6 us -> 41 us (0.962)
  Pallas kernels: 41.9 us -> 40.3 us
    pallas_call x1, Pallas kernels: 41.1 us -> 39.5 us  [per_device(): pl.pallas_call(functools.partial(kernel, (n_dom, n_sub, nx)), out_shape=(...]
where the time goes in v4:
time: 41 us; the launch traced here: 40.9 us
  Pallas kernels  40.3 us (98%)
  between operations  0.64 us (2%)
    pallas_call x1, Pallas kernels, per_device(): pl.pallas_call(functools.partial(kernel, (n_dom, n_sub, nx)), out_shape=(...  39.5 us

profile of v4, /device:TPU:1, one launch (start us, length us, event | category | flops | bytes accessed | tf_op | source)
XLA Modules:
  0.0 40.9 jit_solution(7996959745603781718)
XLA Ops:
  0.6 39.5 %shard_map.104 = (f32[2,32,8,128]{3,2,1,0:T(8,128)S(1)}, f32[2,32,8,128]{3,2,1,0:T(8,128)S(1)}) custom-call(s32[1,1024]{1,0:T(1,128)} %bitcast.2, s32[1,16]{1,0:T(1,128)} %owner_h.1, f32[16]{0:T(128)} %wave_h.1, f32[16]{0:T(128)} %absorb_h.1, f32[16]{0:T(128)} %design_h.1, s32[8,128]{1,0:T(8,128)} %bitcast.3, f32[4,32,8,128]{3,2,1,0:T(8,128)} %fields_h.1, ...), custom_call_target="tpu_custom_call" | custom-call | tf_op jit(solution)/shard_map/pallas_call | solution.py:748
  40.1 0.8 %shard_map.105 = (f32[2,32,8,128]{3,2,1,0:T(8,128)}, f32[2,32,8,128]{3,2,1,0:T(8,128)}) custom-call(f32[2,32,8,128]{3,2,1,0:T(8,128)S(1)} %get-tuple-element.4.forward_v, f32[2,32,8,128]{3,2,1,0:T(8,128)S(1)} %get-tuple-element.5.adjoint_v), custom_call_target="tpu_custom_call" | custom-call | tf_op jit(solution)/shard_map/pallas_call | solution.py:805

commit v5 on v4

--- a/solution.py
+++ b/solution.py
@@ -143,7 +143,7 @@
 
     def trace_copy():
         return pltpu.make_async_remote_copy(
-            src_ref=fields_h.at[:, 0],
+            src_ref=own.at[0, :, 0],
             dst_ref=facing_in,
             send_sem=trace_sem.at[0],
             recv_sem=trace_sem.at[1],
@@ -440,18 +440,19 @@
         lax.fori_loop(0, layers, step, 0, unroll=4)
 
     pl.semaphore_wait(barrier, len(greeted))
+    loads[1].wait()
     trace_copy().start()
     next_copies()[0].start()
-    for load in loads[1:4]:
+    for load in loads[2:4]:
         load.wait()
     loads[4].start()
+    for c in range(4):
+        pack_halo(0, c, lambda l, c=c: own[0, c, l])
+    for copy in halo_copies(0):
+        copy.start()
     pack_halo(0, 4, lambda l: coef[2, 0, l])
     pack_halo(0, 5, lambda l: coef[3, 0, l])
     pack_halo(0, 6, lambda l: labels[l].astype(F32))
-    for copy in halo_copies(0, True):
-        copy.start()
-    for c in range(4):
-        pack_halo(0, c, lambda l, c=c: own[0, c, l])
     for load in small_loads:
         load.wait()
 
@@ -522,7 +523,7 @@
             copy.start()
 
         if it == 0:
-            for copy in halo_copies(0):
+            for copy in halo_copies(0, True):
                 copy.start()
             coefficients_of(0, read=lambda l: labels[l])
             next_copies()[1].start()
@@ -559,6 +560,8 @@
                 stacked[1], turned_block[1, :, columns], contract, preferred_element_type=F32
             )
 
+        if it == 0:
+            trace_copy().wait_send()
         all_jumps(it).wait_recv()
         for i in range(0, n_sub, 4):
             first = [jumps[it, i + t].astype(F32) for t in range(4)]
@@ -675,7 +678,6 @@
                 next_sweep(level, ((0,), (0, 1), (0, 1), (0,))[level], left)
                 sweep_end(level, right, False, final)
         else:
-            trace_copy().wait_send()
             for copy in next_copies():
                 copy.wait_send()
             for k in range(ITERS):
@@ -689,11 +691,12 @@
                     copy.wait_send()
             all_inverses().wait_send()
             ghost_copy(0).wait_send()
+            for level in range(SWEEPS):
+                sweep_end(level, right, False, final)
             ghost_copy(it).wait_recv()
             left = left_ghosts(it)
             for level in range(SWEEPS):
                 sweep_end(level, left, True, final)
-                sweep_end(level, right, False, final)
             ghost_copy(it).wait_send()
 
 

time: 41 us -> 39.7 us (0.968)
  Pallas kernels: 40.3 us -> 39 us
    pallas_call x1, Pallas kernels: 39.5 us -> 38.1 us  [per_device(): pl.pallas_call(functools.partial(kernel, (n_dom, n_sub, nx)), out_shape=(...]
where the time goes in v5:
time: 39.7 us; the launch traced here: 39.6 us
  Pallas kernels  39 us (98%)
  between operations  0.64 us (2%)
    pallas_call x1, Pallas kernels, per_device(): pl.pallas_call(functools.partial(kernel, (n_dom, n_sub, nx)), out_shape=(...  38.1 us
    pallas_call x1, Pallas kernels, per_device(): pl.pallas_call(store_kernel, out_shape=(out, out), in_specs=[vmem, vmem],...  0.81 us

profile of v5, /device:TPU:1, one launch (start us, length us, event | category | flops | bytes accessed | tf_op | source)
XLA Modules:
  0.0 39.6 jit_solution(11094937139223139828)
XLA Ops:
  0.6 38.1 %shard_map.104 = (f32[2,32,8,128]{3,2,1,0:T(8,128)S(1)}, f32[2,32,8,128]{3,2,1,0:T(8,128)S(1)}) custom-call(s32[1,1024]{1,0:T(1,128)} %bitcast.2, s32[1,16]{1,0:T(1,128)} %owner_h.1, f32[16]{0:T(128)} %wave_h.1, f32[16]{0:T(128)} %absorb_h.1, f32[16]{0:T(128)} %design_h.1, s32[8,128]{1,0:T(8,128)} %bitcast.3, f32[4,32,8,128]{3,2,1,0:T(8,128)} %fields_h.1, ...), custom_call_target="tpu_custom_call" | custom-call | tf_op jit(solution)/shard_map/pallas_call | solution.py:751
  38.8 0.8 %shard_map.105 = (f32[2,32,8,128]{3,2,1,0:T(8,128)}, f32[2,32,8,128]{3,2,1,0:T(8,128)}) custom-call(f32[2,32,8,128]{3,2,1,0:T(8,128)S(1)} %get-tuple-element.4.forward_v, f32[2,32,8,128]{3,2,1,0:T(8,128)S(1)} %get-tuple-element.5.adjoint_v), custom_call_target="tpu_custom_call" | custom-call | tf_op jit(solution)/shard_map/pallas_call | solution.py:808

commit v6 on v5

--- a/solution.py
+++ b/solution.py
@@ -165,8 +165,8 @@
                 pltpu.make_async_remote_copy(
                     src_ref=src,
                     dst_ref=dst,
-                    send_sem=nxt_send.at[k],
-                    recv_sem=nxt_recv.at[k],
+                    send_sem=nxt_send.at[k % 2],
+                    recv_sem=nxt_recv.at[k % 2],
                     device_id=(before_d, me_s),
                     device_id_type=MESH,
                 )
@@ -224,6 +224,12 @@
     def all_sides(it):
         return all_of(side_in.at[it], side_send.at[it], side_recv.at[it])
 
+    def all_next():
+        return [
+            all_of(nxt.at[0], nxt_send.at[0], nxt_recv.at[0]),
+            all_of(nxt_coef, nxt_send.at[1], nxt_recv.at[1]),
+        ]
+
     def all_inverses():
         return all_of(inv_in, inv_send, inv_recv)
 
@@ -270,8 +276,8 @@
                 pltpu.make_async_remote_copy(
                     src_ref=halo_out.at[part],
                     dst_ref=halo_in.at[part],
-                    send_sem=halo_send.at[2 * it + second],
-                    recv_sem=halo_recv.at[2 * it + second],
+                    send_sem=halo_send.at[it * (1 + second)],
+                    recv_sem=halo_recv.at[it * (1 + second)],
                     device_id=(me_d, sub),
                     device_id_type=MESH,
                 )
@@ -279,8 +285,9 @@
         return copies
 
     def all_halos(it, second=False):
-        part = (pl.ds(2 * it, 2),) + halo_part(it, second)
-        return all_of(halo_in.at[part], halo_send.at[2 * it + second], halo_recv.at[2 * it + second])
+        rest = halo_part(it, second) if it else (pl.ds(0, halo_in.shape[1]), pl.ds(0, halo_in.shape[2]))
+        k = it * (1 + second)
+        return all_of(halo_in.at[(pl.ds(2 * it, 2),) + rest], halo_send.at[k], halo_recv.at[k])
 
     half = layers // 2
 
@@ -597,7 +604,6 @@
             products[it, 0, k] = outgoing[it, me_s + k]
 
         if it == 0:
-            all_halos(it, True).wait_recv()
             all_halos(it).wait_recv()
             unpack_fields(it, 0, half // 2)
             for c in range(2):
@@ -631,7 +637,7 @@
                 copy.start()
 
         if not final:
-            for copy in next_copies():
+            for copy in all_next():
                 copy.wait_recv()
             next_sweep(0, range(1, depth - 1), None)
             next_sweep(1, range(2, depth - 2), None)
@@ -678,7 +684,7 @@
                 next_sweep(level, ((0,), (0, 1), (0, 1), (0,))[level], left)
                 sweep_end(level, right, False, final)
         else:
-            for copy in next_copies():
+            for copy in all_next():
                 copy.wait_send()
             for k in range(ITERS):
                 for copy in (
@@ -686,9 +692,9 @@
                     all_products(k),
                     all_sides(k),
                     all_halos(k),
-                    all_halos(k, True),
                 ):
                     copy.wait_send()
+            all_halos(1, True).wait_send()
             all_inverses().wait_send()
             ghost_copy(0).wait_send()
             for level in range(SWEEPS):
@@ -793,13 +799,13 @@
                 dma((ITERS,)),
                 dma(()),
                 dma(()),
-                dma((2 * ITERS,)),
-                dma((2 * ITERS,)),
+                dma((3,)),
+                dma((3,)),
                 pltpu.VMEM((2, 2, 4, SWEEPS + 1, 8, 128), F32),
                 pltpu.VMEM((5, 2, SWEEPS, 8, 128), F32),
                 pltpu.VMEM((4, SWEEPS + 1, 8, 128), F32),
-                dma((4,)),
-                dma((4,)),
+                dma((2,)),
+                dma((2,)),
             ],
             compiler_params=pltpu.CompilerParams(
                 collective_id=0, has_side_effects=True, vmem_limit_bytes=20 * 1024 * 1024

time: 39.7 us -> 39.6 us (level)
  no operation moved by 1% of the time
where the time goes in v6:
time: 39.6 us; the launch traced here: 39.5 us
  Pallas kernels  38.9 us (98%)
  between operations  0.64 us (2%)
    pallas_call x1, Pallas kernels, per_device(): pl.pallas_call(functools.partial(kernel, (n_dom, n_sub, nx)), out_shape=(...  38.1 us
    pallas_call x1, Pallas kernels, per_device(): pl.pallas_call(store_kernel, out_shape=(out, out), in_specs=[vmem, vmem],...  0.81 us

profile of v6, /device:TPU:1, one launch (start us, length us, event | category | flops | bytes accessed | tf_op | source)
XLA Modules:
  0.0 39.5 jit_solution(2885447808454650470)
XLA Ops:
  0.6 38.1 %shard_map.104 = (f32[2,32,8,128]{3,2,1,0:T(8,128)S(1)}, f32[2,32,8,128]{3,2,1,0:T(8,128)S(1)}) custom-call(s32[1,1024]{1,0:T(1,128)} %bitcast.2, s32[1,16]{1,0:T(1,128)} %owner_h.1, f32[16]{0:T(128)} %wave_h.1, f32[16]{0:T(128)} %absorb_h.1, f32[16]{0:T(128)} %design_h.1, s32[8,128]{1,0:T(8,128)} %bitcast.3, f32[4,32,8,128]{3,2,1,0:T(8,128)} %fields_h.1, ...), custom_call_target="tpu_custom_call" | custom-call | tf_op jit(solution)/shard_map/pallas_call | solution.py:757
  38.7 0.8 %shard_map.105 = (f32[2,32,8,128]{3,2,1,0:T(8,128)}, f32[2,32,8,128]{3,2,1,0:T(8,128)}) custom-call(f32[2,32,8,128]{3,2,1,0:T(8,128)S(1)} %get-tuple-element.4.forward_v, f32[2,32,8,128]{3,2,1,0:T(8,128)S(1)} %get-tuple-element.5.adjoint_v), custom_call_target="tpu_custom_call" | custom-call | tf_op jit(solution)/shard_map/pallas_call | solution.py:814
